TPU v7x, 128 devices: a whole 4x4x4 slice. The times are simulated.
128 devices in a mesh: aux: 8 (over y, x_hi), pair: 16 (over x_lo, z, core).
Axes of the slice: x: 4 (x_hi: 2, x_lo: 2; x = x_hi * 2 + x_lo), y: 4, z: 4, core: 2. Of those that a mesh axis runs over, the one named last changes fastest.
Arguments:
- three_centre: bfloat16 [32, 128, 8, 64, 512], P('pair', 'aux'), may hold values from -6 to 6
- slot_groups: int32 [32, 128], P('pair', 'aux'), may hold values from 0 to 127, as said below
- slot_count: int32 [32, 8], P('pair', 'aux'), may hold values from 1 to 16, as said below
- block_cost: int32 [32, 128], P('pair', 'aux'), may hold values from 1 to 4
- green_occ: bfloat16 [32, 512, 128], P('pair'), may hold values from -0.25 to 0.25
- green_vir: bfloat16 [32, 64, 128], P('pair'), may hold values from -0.75 to 0.75
- target: bfloat16 [1024, 32, 128, 128], P(None, 'pair', 'aux'), may hold values from -0.0390625 to 0.0390625
Outputs:
- response: float32 [1024, 1024], P('aux', 'pair')
Inputs may be any that keep to these rules, and one draw needn't show every extreme that they name: Each row of slot_groups is a permutation of 0 to 127. `slot_count`: in every orbital block some device has all its slots live.
All inputs are finite; a program needn't handle non-finite values.
Results may differ from a plain program's by a relative error of at most 0.0041.
Values may be sent and summed in bfloat16 or wider, within the bound.
No kernel may reach another device: no remote copies, remote signals or barrier semaphores. Data moves between devices by JAX's collectives and lax.ppermute only.
A program may use at most 128 MiB of HBM per device.

v0:
```python
import functools

import jax
import jax.numpy as jnp
from jax import lax
from jax.experimental import pallas as pl
from jax.experimental.pallas import tpu as pltpu
from jax.sharding import PartitionSpec as P


NAUX = 1024
AUXG = 8
MU = 512
NU = 64
LAM = 128
SIG = 128
MUC = 128
NGROUPS = 128
DEPTH = 4
BF16 = jnp.bfloat16
F32 = jnp.float32
STAGES = ((0, 2, 6, 1, 5), (3, 7, 4))


def fold(low, first, second):
    return (
        jnp.where(low, first, pltpu.roll(second, 64, 1)),
        jnp.where(low, pltpu.roll(first, 64, 1), second),
    )


def half_kernel(dests, count, cost, group, me, x_hbm, occ, *rest):
    outs, (xbuf, turned, sem) = rest[:dests], rest[dests:]
    blocks, slots = cost.shape
    lam_each = LAM // dests
    units = MU // MUC
    first = count[0]
    total = first + count[1]

    def place(i):
        b = jnp.where(i < first, 0, 1)
        return b, i - b * first

    def copy(i, k):
        b, s = place(i)
        slot = lax.rem(i, DEPTH)
        return pltpu.make_async_copy(
            x_hbm.at[b, s, :, :, pl.ds(0, MUC * k)],
            xbuf.at[slot, :, :, pl.ds(0, MUC * k)],
            sem.at[slot],
        )

    def issue(i):
        b, s = place(i)
        c = cost[b, s]
        for k in range(1, units + 1):
            @pl.when(c == k)
            def _(k=k):
                copy(i, k).start()

    for i in range(DEPTH - 1):
        @pl.when(i < total)
        def _(i=i):
            issue(i)

    shape = (lam_each, 128)
    row = lax.broadcasted_iota(jnp.int32, shape, 0)
    lane = lax.broadcasted_iota(jnp.int32, shape, 1)
    head = jnp.zeros(shape, jnp.int32)
    for b in range(blocks):
        head = jnp.where((row == b) & (lane == slots), count[b], head)
        for s in range(slots):
            head = jnp.where((row == b) & (lane == s), group[b, s], head)
    head = head.astype(F32).astype(BF16)
    for out in outs:
        out[blocks * slots * lam_each:, 0:128] = head
    old = lax.broadcasted_iota(jnp.int32, (LAM, LAM), 0)
    new = lax.broadcasted_iota(jnp.int32, (LAM, LAM), 1)
    moves = old == (me[0] ^ (new // lam_each)) * lam_each + lax.rem(new, lam_each)
    moves = jnp.where(moves, 1.0, 0.0).astype(BF16)
    for b in range(blocks):
        turned[b] = jnp.dot(occ[b], moves, preferred_element_type=F32).astype(BF16)

    def step(i, carry):
        b, s = place(i)
        slot = lax.rem(i, DEPTH)

        @pl.when(i + DEPTH - 1 < total)
        def _():
            issue(i + DEPTH - 1)

        c = cost[b, s]
        for k in range(1, units + 1):
            @pl.when(c == k)
            def _(k=k):
                copy(i, k).wait()
                x = xbuf[slot, :, :, 0:MUC * k].reshape(AUXG * NU, MUC * k)
                h = jnp.dot(x, turned[b, 0:MUC * k, :], preferred_element_type=F32)
                ht = h.T.astype(BF16)
                at = pl.multiple_of((b * slots + s) * lam_each, lam_each)
                for d in range(dests):
                    outs[d][pl.ds(at, lam_each), :] = ht[d * lam_each:(d + 1) * lam_each]
        return carry

    lax.fori_loop(0, total, step, 0)


ROWS = NAUX + 32


def response_kernel(sources, last, *rest):
    if last:
        core, rest = rest[0], rest[1:]
    parts, rest = rest[:sources], rest[sources:]
    if last:
        before, columns, keep_ref, send_ref, z, lhs, acc, headint, table, order, ssem, r = rest
    else:
        columns, r, z, lhs, acc, headint, table, order, ssem = rest
    blocks, _, width = columns.shape
    pairs = width // 128
    lam_each = 2 * pairs
    slots = (parts[0].shape[0] - lam_each) // (blocks * lam_each)
    block_rows = 256
    held = block_rows // AUXG

    for s in range(sources):
        rows = parts[s][blocks * slots * lam_each:, 0:128]
        headint[s] = rows.astype(F32).astype(jnp.int32)[0:8]
    to_scalar = pltpu.make_async_copy(headint, table, ssem.at[0])
    to_scalar.start()
    r[...] = before[...] if last else jnp.zeros_like(r)
    low = lax.broadcasted_iota(jnp.int32, (8, 128), 1) < 64
    to_scalar.wait()
    for b in range(blocks):
        filled = jnp.int32(0)
        for s in range(sources):
            n = table[s, b, slots]

            def spread(ch, carry, s=s, b=b, filled=filled):
                start = pl.multiple_of((b * slots + ch * 4) * lam_each, 4 * lam_each)
                four = parts[s][pl.ds(start, 4 * lam_each), :].astype(F32)
                for i in range(4):
                    at = filled + ch * 4 + i
                    order[at] = table[s, b, ch * 4 + i]
                    for j in range(AUXG // 2):
                        cols = slice(128 * j, 128 * (j + 1))
                        upper = four[i * lam_each:i * lam_each + pairs, cols]
                        lower = four[i * lam_each + pairs:(i + 1) * lam_each, cols]
                        for e, v in enumerate(fold(low, upper, lower)):
                            z[pl.ds(at * AUXG + 2 * j + e, pairs, stride=ROWS), :] = v
                return carry

            lax.fori_loop(0, (n + 3) // 4, spread, 0)
            filled = filled + n

        def multiply(m, carry, b=b, filled=filled):
            for q in range(pairs):
                start = pl.multiple_of(q * ROWS + m * block_rows, 8)
                lhs[:, q * 128:(q + 1) * 128] = z[pl.ds(start, block_rows), :].astype(BF16)
            acc[...] = lax.dot_general(
                lhs[...], columns[b], (((1,), (1,)), ((), ())), preferred_element_type=F32,
            )

            def scatter(i, inner):
                g = order[m * held + i]
                to = pl.ds(pl.multiple_of(g * AUXG, AUXG), AUXG)
                at = pl.ds(pl.multiple_of(i * AUXG, AUXG), AUXG)
                for q in range(r.shape[0]):
                    r[q, to, :] += acc[at, q * 128:(q + 1) * 128]
                return inner

            lax.fori_loop(0, jnp.minimum(held, filled - m * held), scatter, 0)
            return carry

        lax.fori_loop(0, (filled + held - 1) // held, multiply, 0)

    if last:
        is_first = core[0] == 0
        low = lax.broadcasted_iota(jnp.int32, (64, 128), 1) < 64
        for a in range(keep_ref.shape[0]):
            for q in range(keep_ref.shape[1]):
                even, odd = fold(
                    low, r[q, a * 128:a * 128 + 64, :], r[q, a * 128 + 64:a * 128 + 128, :])
                keep_ref[a, q] = jnp.where(is_first, even, odd)
                send_ref[a, q] = jnp.where(is_first, odd, even).astype(BF16)


def local(three_centre, slot_groups, slot_count, block_cost, green_occ, green_vir, target):
    blocks, slots = slot_groups.shape
    dests = lax.axis_size("aux")
    chips = lax.axis_size("chip")
    lam_each = LAM // dests
    pairs = lam_each // 2
    smem = pl.BlockSpec(memory_space=pltpu.SMEM)
    vmem = pl.BlockSpec(memory_space=pltpu.VMEM)
    hbm = pl.BlockSpec(memory_space=pltpu.MemorySpace.HBM)

    held = (blocks * slots + 1) * lam_each
    sent = pl.pallas_call(
        functools.partial(half_kernel, dests),
        out_shape=[jax.ShapeDtypeStruct((held, AUXG * NU), BF16)] * dests,
        in_specs=[smem, smem, smem, smem, hbm, vmem],
        out_specs=[vmem] * dests,
        scratch_shapes=[
            pltpu.VMEM((DEPTH, AUXG, NU, MU), BF16),
            pltpu.VMEM((blocks, MU, LAM), BF16),
            pltpu.SemaphoreType.DMA((DEPTH,)),
        ],
        cost_estimate=pl.CostEstimate(flops=2 * 10**9, bytes_accessed=2 * 10**7, transcendentals=0),
        name="half",
    )(slot_count.reshape(-1), block_cost, slot_groups, lax.axis_index("aux").reshape(1),
      three_centre, green_occ)
    arrived = {0: sent[0]}
    for stage in STAGES:
        for d in stage:
            if d:
                arrived[d] = lax.ppermute(sent[d], "aux", [(i, i ^ d) for i in range(dests)])

    columns = jnp.einsum(
        "qbzit,bnt->bqizn", target.reshape(NAUX, blocks, 2, pairs, SIG), green_vir,
        preferred_element_type=F32,
    ).astype(BF16).reshape(blocks, NAUX, pairs * 128)
    core = lax.axis_index("core").reshape(1)
    running = None
    for number, stage in enumerate(STAGES):
        last = number == len(STAGES) - 1
        inputs = [arrived[d] for d in stage]
        specs = [vmem] * len(stage)
        whole = jax.ShapeDtypeStruct((NAUX // 128, NAUX, 128), F32)
        scratch = [
            pltpu.VMEM((pairs * ROWS, 128), F32),
            pltpu.VMEM((256, pairs * 128), BF16),
            pltpu.VMEM((256, NAUX), F32),
            pltpu.VMEM((len(stage), 8, 128), jnp.int32),
            pltpu.SMEM((len(stage), 8, 128), jnp.int32),
            pltpu.SMEM((NGROUPS + 4,), jnp.int32),
            pltpu.SemaphoreType.DMA((1,)),
        ]
        shape = whole
        if last:
            inputs = [core, *inputs, running]
            specs = [smem, *specs, vmem]
            scratch.append(pltpu.VMEM(whole.shape, F32))
            shape = (
                jax.ShapeDtypeStruct((dests, chips, 64, 128), F32),
                jax.ShapeDtypeStruct((dests, chips, 64, 128), BF16),
            )
        respond = pl.pallas_call(
            functools.partial(response_kernel, len(stage), last),
            out_shape=shape,
            in_specs=[*specs, vmem],
            out_specs=(vmem, vmem) if last else vmem,
            scratch_shapes=scratch,
            compiler_params=pltpu.CompilerParams(vmem_limit_bytes=24 * 2**20),
            cost_estimate=pl.CostEstimate(flops=3 * 10**9, bytes_accessed=10**7, transcendentals=0),
        )
        running = respond(*inputs, columns)
    keep, send = running
    other = lax.ppermute(send, "core", [(0, 1), (1, 0)])
    mine = (keep + other.astype(F32)).astype(BF16).reshape(dests * chips, 64, 128)
    parts = lax.all_to_all(mine, ("aux", "chip"), split_axis=0, concat_axis=0, tiled=True)
    total = jnp.sum(parts.astype(F32), axis=0)
    return jnp.concatenate([total[:, :64], total[:, 64:]], axis=0)


def solution(mesh):
    aux, pair = mesh.devices.shape
    fine = jax.sharding.Mesh(
        mesh.devices.reshape(aux, pair // 2, 2), ("aux", "chip", "core")
    )
    both = ("chip", "core")
    in_specs = (
        P(both, "aux", None, None, None),
        P(both, "aux"),
        P(both, "aux"),
        P(both, "aux"),
        P(both, None, None),
        P(both, None, None),
        P(None, both, "aux", None),
    )

    return jax.shard_map(local, mesh=fine, in_specs=in_specs, out_specs=P("aux", both), check_vma=False)
```

profile of v0, /device:TPU:0, one launch (start us, length us, event | category | flops | bytes accessed | tf_op | source)
XLA Modules:
  0.0 129.7 jit_solution(15976243421977022976)
XLA Ops:
  0.0 0.0 copy-start
  0.0 13.4 %half.1 = (bf16[528,512]{1,0:T(8,128)(2,1)}, bf16[528,512]{1,0:T(8,128)(2,1)}, bf16[528,512]{1,0:T(8,128)(2,1)}, bf16[528,512]{1,0:T(8,128)(2,1)}, bf16[528,512]...) custom-call(s32[2]{0:T(128)} %bitcast.16, s32[2,16]{1,0:T(2,128)} %cost.1, ...), custom_call_target="tpu_custom_call" | custom-call | flops 2000000000 | bytes 20000000 | tf_op jit(solution)/shard_map/half/pallas_call | solution.py:199
  13.4 0.1 collective-permute-start.3
  13.5 0.1 collective-permute-start.4
  13.6 4.0 %collective-permute-start = (bf16[528,512]{1,0:T(8,128)(2,1)}, bf16[528,512]{1,0:T(8,128)(2,1)S(1)}, u32[]{:S(2)}, u32[]{:S(2)}) collective-permute-start(bf16[528,512]{1,0:T(8,128)(2,1)} %get-tuple-element.15), channel_id=1, source_target_pairs={{0,48},{16,32},{32,16},{48,0},{64,112},{80,96},{96,80},{112,64},{1... | collective-permute-start | bytes 1622024 | tf_op jit(solution)/shard_map/ppermute | solution.py:217
  17.6 3.0 %collective-permute-start.1 = (bf16[528,512]{1,0:T(8,128)(2,1)}, bf16[528,512]{1,0:T(8,128)(2,1)S(1)}, u32[]{:S(2)}, u32[]{:S(2)}) collective-permute-start(bf16[528,512]{1,0:T(8,128)(2,1)} %get-tuple-element.16), channel_id=1, source_target_pairs={{0,112},{16,96},{32,80},{48,64},{64,48},{80,32},{96,16},{112,0},{1... | collective-permute-start | bytes 1622024 | tf_op jit(solution)/shard_map/ppermute | solution.py:217
  20.6 0.0 collective-permute-start.2
  20.6 21.5 %collective-permute-done.3.rest_1_ = bf16[528,512]{1,0:T(8,128)(2,1)S(1)} collective-permute-done((bf16[528,512]{1,0:T(8,128)(2,1)}, bf16[528,512]{1,0:T(8,128)(2,1)S(1)}, u32[]{:S(2)}, u32[]{:S(2)}) %collective-permute-start.3) | collective-permute-done | bytes 540704 | tf_op jit(solution)/shard_map/ppermute | solution.py:217
  42.0 0.0 collective-permute-start.5
  42.0 0.0 collective-permute-done.4.rest_2_
  42.0 0.5 collective-permute-start.6
  42.6 0.0 copy-done
  42.6 14.7 %convert_bitcast_fusion = bf16[2,1024,8,2,64]{1,4,2,3,0:T(8,128)(2,1)} fusion(bf16[1024,2,2,8,128]{4,3,2,1,0:T(8,128)(2,1)} %bitcast.14, bf16[2,64,128]{2,1,0:T(8,128)(2,1)S(1)} %copy-done), kind=kOutput, calls=%fused_computation.2 | convolution fusion | flops 538968064 | bytes 12615680 | tf_op jit(solution)/shard_map/qbzit,bnt->bqizn/dot_general | solution.py:219
  57.3 4.9 %copy.15 = bf16[2,1024,8,2,64]{1,4,3,2,0:T(8,128)(2,1)} copy(bf16[2,1024,8,2,64]{1,4,2,3,0:T(8,128)(2,1)} %convert_bitcast_fusion) | data formatting | bytes 8388608 | tf_op jit(solution)/shard_map/convert_element_type | solution.py:222
  62.1 6.2 %copy.16.rest_5_ = bf16[2,1024,1024]{2,1,0:T(8,128)(2,1)} copy(bf16[2,1024,1024]{1,2,0:T(8,128)(2,1)} %bitcast.13) | data formatting | bytes 8388608 | tf_op jit(solution)/shard_map/reshape | solution.py:222
  68.4 0.0 collective-permute-done.5.rest_3_
  68.4 0.0 collective-permute-done.6.rest_4_
  68.4 0.0 copy-done.3
  68.4 0.0 copy-start.1
  68.4 2.2 %copy-done.1 = bf16[2,1024,1024]{2,1,0:T(8,128)(2,1)S(1)} copy-done((bf16[2,1024,1024]{2,1,0:T(8,128)(2,1)S(1)}, bf16[2,1024,1024]{2,1,0:T(8,128)(2,1)}, u32[]{:S(2)}) %copy-start.1) | copy-done | bytes 4194328
  70.6 8.3 %shard_map.73.rest_4_ = f32[8,1024,128]{2,1,0:T(8,128)S(1)} custom-call(bf16[528,512]{1,0:T(8,128)(2,1)S(1)} %copy-done.3, bf16[528,512]{1,0:T(8,128)(2,1)S(1)} %collective-permute-done.3.rest_1_, bf16[528,512]{1,0:T(8,128)(2,1)S(1)} %collective-permute-done.4.rest_2_, bf16[528,512]{1,0:T(8,128)(2,1)} %collective-permute-done.5.rest_3_, ...), custom_call_target="tpu_custom_call" | custom-call | flops 3000000000 | bytes 10000000 | tf_op jit(solution)/shard_map/pallas_call | solution.py:257
  78.9 0.0 collective-permute-done.rest_1_
  79.0 0.0 collective-permute-done.1.rest_2_
  79.0 0.0 collective-permute-done.2.rest_3_
  79.0 5.4 %shard_map.74 = (f32[8,8,64,128]{3,2,1,0:T(8,128)S(1)}, bf16[8,8,64,128]{3,2,1,0:T(8,128)(2,1)S(1)}) custom-call(s32[1]{0:T(128)} %bitcast.rest_0_, bf16[528,512]{1,0:T(8,128)(2,1)S(1)} %collective-permute-done.rest_1_, bf16[528,512]{1,0:T(8,128)(2,1)S(1)} %collective-permute-done.1.rest_2_, bf16[528,512]{1,0:T(8,128)(2,1)S(1)} %collective-permute-done.2.rest_3_, ...), custom_call_target="tpu_custom_call" | custom-call | flops 3000000000 | bytes 10000000 | tf_op jit(solution)/shard_map/pallas_call | solution.py:257
  84.3 0.1 collective-permute-start.7
  84.4 2.6 %collective-permute-done.7 = bf16[8,8,64,128]{3,2,1,0:T(8,128)(2,1)S(1)} collective-permute-done((bf16[8,8,64,128]{3,2,1,0:T(8,128)(2,1)S(1)}, bf16[8,8,64,128]{3,2,1,0:T(8,128)(2,1)S(1)}, u32[]{:S(2)}, u32[]{:S(2)}) %collective-permute-start.7) | collective-permute-done | bytes 1048608 | tf_op jit(solution)/shard_map/ppermute | solution.py:259
  87.1 0.4 add_convert_fusion
  87.5 41.3 %all_to_all.5 = bf16[64,64,128]{2,1,0:T(8,128)(2,1)S(1)} all-to-all(bf16[64,64,128]{2,1,0:T(8,128)(2,1)S(1)} %bitcast.15), channel_id=1, replica_groups=mesh['aux'=8,'chip'=8,'core'=2] {'aux','chip'}, dimensions={0} | all-to-all | bytes 2097152 | tf_op jit(solution)/shard_map/all_to_all | solution.py:261
  128.8 0.2 convert_reduce_fusion
  129.0 0.1 fusion.5
  129.0 0.7 copy.18
  (4 shorter events, 0.0 us)
Async XLA Ops:
  0.0 42.6 %copy-start = (bf16[2,64,128]{2,1,0:T(8,128)(2,1)S(1)}, bf16[2,64,128]{2,1,0:T(8,128)(2,1)}, u32[]{:S(2)}) copy-start(bf16[2,64,128]{2,1,0:T(8,128)(2,1)} %param.12) | copy-start | bytes 98308
  13.4 28.6 %collective-permute-start.3 = (bf16[528,512]{1,0:T(8,128)(2,1)}, bf16[528,512]{1,0:T(8,128)(2,1)S(1)}, u32[]{:S(2)}, u32[]{:S(2)}) collective-permute-start(bf16[528,512]{1,0:T(8,128)(2,1)} %get-tuple-element.19), channel_id=1, source_target_pairs={{0,32},{16,48},{32,0},{48,16},{64,96},{80,112},{96,64},{112,80},{1... | collective-permute-start | bytes 1622024 | tf_op jit(solution)/shard_map/ppermute | solution.py:217
  13.5 28.5 %collective-permute-start.4 = (bf16[528,512]{1,0:T(8,128)(2,1)}, bf16[528,512]{1,0:T(8,128)(2,1)S(1)}, u32[]{:S(2)}, u32[]{:S(2)}) collective-permute-start(bf16[528,512]{1,0:T(8,128)(2,1)} %get-tuple-element.20), channel_id=1, source_target_pairs={{0,96},{16,112},{32,64},{48,80},{64,32},{80,48},{96,0},{112,16},{1... | collective-permute-start | bytes 1622024 | tf_op jit(solution)/shard_map/ppermute | solution.py:217
  13.6 65.3 %collective-permute-start = (bf16[528,512]{1,0:T(8,128)(2,1)}, bf16[528,512]{1,0:T(8,128)(2,1)S(1)}, u32[]{:S(2)}, u32[]{:S(2)}) collective-permute-start(bf16[528,512]{1,0:T(8,128)(2,1)} %get-tuple-element.15), channel_id=1, source_target_pairs={{0,48},{16,32},{32,16},{48,0},{64,112},{80,96},{96,80},{112,64},{1... | collective-permute-start | bytes 1622024 | tf_op jit(solution)/shard_map/ppermute | solution.py:217
  17.6 61.3 %collective-permute-start.1 = (bf16[528,512]{1,0:T(8,128)(2,1)}, bf16[528,512]{1,0:T(8,128)(2,1)S(1)}, u32[]{:S(2)}, u32[]{:S(2)}) collective-permute-start(bf16[528,512]{1,0:T(8,128)(2,1)} %get-tuple-element.16), channel_id=1, source_target_pairs={{0,112},{16,96},{32,80},{48,64},{64,48},{80,32},{96,16},{112,0},{1... | collective-permute-start | bytes 1622024 | tf_op jit(solution)/shard_map/ppermute | solution.py:217
  20.6 58.4 %collective-permute-start.2 = (bf16[528,512]{1,0:T(8,128)(2,1)}, bf16[528,512]{1,0:T(8,128)(2,1)S(1)}, u32[]{:S(2)}, u32[]{:S(2)}) collective-permute-start(bf16[528,512]{1,0:T(8,128)(2,1)} %get-tuple-element.17), channel_id=1, source_target_pairs={{0,64},{16,80},{32,96},{48,112},{64,0},{80,16},{96,32},{112,48},{1... | collective-permute-start | bytes 1622024 | tf_op jit(solution)/shard_map/ppermute | solution.py:217
  42.0 26.4 %collective-permute-start.5 = (bf16[528,512]{1,0:T(8,128)(2,1)}, bf16[528,512]{1,0:T(8,128)(2,1)}, u32[]{:S(2)}, u32[]{:S(2)}) collective-permute-start(bf16[528,512]{1,0:T(8,128)(2,1)} %get-tuple-element.21), channel_id=1, source_target_pairs={{0,16},{16,0},{32,48},{48,32},{64,80},{80,64},{96,112},{112,96},{1... | collective-permute-start | bytes 1622024 | tf_op jit(solution)/shard_map/ppermute | solution.py:217
  42.0 26.4 %collective-permute-start.6 = (bf16[528,512]{1,0:T(8,128)(2,1)}, bf16[528,512]{1,0:T(8,128)(2,1)}, u32[]{:S(2)}, u32[]{:S(2)}) collective-permute-start(bf16[528,512]{1,0:T(8,128)(2,1)} %get-tuple-element.22), channel_id=1, source_target_pairs={{0,80},{16,64},{32,112},{48,96},{64,16},{80,0},{96,48},{112,32},{1... | collective-permute-start | bytes 1622024 | tf_op jit(solution)/shard_map/ppermute | solution.py:217
  62.1 6.3 %copy-start.3 = (bf16[528,512]{1,0:T(8,128)(2,1)S(1)}, bf16[528,512]{1,0:T(8,128)(2,1)}, u32[]{:S(2)}) copy-start(bf16[528,512]{1,0:T(8,128)(2,1)} %get-tuple-element.18.rest_0_) | copy-start | bytes 1622020
  68.4 2.2 %copy-start.1 = (bf16[2,1024,1024]{2,1,0:T(8,128)(2,1)S(1)}, bf16[2,1024,1024]{2,1,0:T(8,128)(2,1)}, u32[]{:S(2)}) copy-start(bf16[2,1024,1024]{2,1,0:T(8,128)(2,1)} %copy.16.rest_5_) | copy-start | bytes 12582916
  70.6 8.4 %copy-start.2 = (bf16[2,1024,1024]{2,1,0:T(8,128)(2,1)S(1)}, bf16[2,1024,1024]{2,1,0:T(8,128)(2,1)}, u32[]{:S(2)}) copy-start(bf16[2,1024,1024]{2,1,0:T(8,128)(2,1)} %copy.16.rest_5_) | copy-start | bytes 12582916
  84.3 2.7 %collective-permute-start.7 = (bf16[8,8,64,128]{3,2,1,0:T(8,128)(2,1)S(1)}, bf16[8,8,64,128]{3,2,1,0:T(8,128)(2,1)S(1)}, u32[]{:S(2)}, u32[]{:S(2)}) collective-permute-start(bf16[8,8,64,128]{3,2,1,0:T(8,128)(2,1)S(1)} %get-tuple-element.24), channel_id=1, source_target_pairs={{0,1},{1,0},{2,3},{3,2},{4,5},{5,4},{6,7},{7,6},{8,9},{9,8},{10,11... | collective-permute-start | bytes 3145736 | tf_op jit(solution)/shard_map/ppermute | solution.py:259
where the time goes:
time: 130 us
  blocking collectives  41.3 us (32%)
  Pallas kernels  27.1 us (21%)
  waiting for transfers between devices  24.1 us (19%)
  matrix products  14.7 us (11%)
  local copies, waits for them, and re-layouts  14.1 us (11%)
  starting transfers between devices  7.76 us (6%)
    all_to_all x1, blocking collectives, local(): lax.all_to_all(mine, ('aux', 'chip'), split_axis=0, concat_axis=0, tiled=...  41.3 us
    ppermute x7, waiting for transfers between devices, local(): lax.ppermute(sent[d], 'aux', [(i, i ^ d) for i in range(dests)])  21.5 us
    dot_general x1, matrix products, local(): jnp.einsum('qbzit,bnt->bqizn', target.reshape(NAUX, blocks, 2, pairs, SIG...  14.7 us
    pallas_call x2, Pallas kernels, local(): running = respond(*inputs, columns)  13.7 us
    pallas_call x1, Pallas kernels, local(): pl.pallas_call(functools.partial(half_kernel, dests), out_shape=[jax.Shap...  13.4 us
    ppermute x7, starting transfers between devices, local(): lax.ppermute(sent[d], 'aux', [(i, i ^ d) for i in range(dests)])  7.68 us
    reshape x1, local copies, waits for them, and re-layouts, local(): columns = jnp.einsum('qbzit,bnt->bqizn', target.reshape(NAUX, blocks, 2,...  6.25 us
    convert_element_type x1, local copies, waits for them, and re-layouts, local(): columns = jnp.einsum('qbzit,bnt->bqizn', target.reshape(NAUX, blocks, 2,...  4.86 us
  transfers between devices with their start and end apart: 8, of which 2 were waited for; matrix products, arithmetic and copies ran while one was open for 20% of the time, Pallas kernels for 6%

commit v1 on v0

--- a/solution.py
+++ b/solution.py
@@ -16,10 +16,10 @@
 SIG = 128
 MUC = 128
 NGROUPS = 128
-DEPTH = 4
+DEPTH = 6
 BF16 = jnp.bfloat16
 F32 = jnp.float32
-STAGES = ((0, 2, 6, 1, 5), (3, 7, 4))
+STAGES = ((0, 1, 2, 5, 6, 3, 4), (7,))
 
 
 def fold(low, first, second):
@@ -50,18 +50,19 @@
             sem.at[slot],
         )
 
+    def each_size(i, act):
+        b, s = place(i)
+        c = jnp.where(i < DEPTH, units, cost[b, s])
+        for k in range(1, units + 1):
+            @pl.when((c == k) & (i < total))
+            def _(k=k):
+                act(copy(i, k))
+
     def issue(i):
-        b, s = place(i)
-        c = cost[b, s]
-        for k in range(1, units + 1):
-            @pl.when(c == k)
-            def _(k=k):
-                copy(i, k).start()
-
-    for i in range(DEPTH - 1):
-        @pl.when(i < total)
-        def _(i=i):
-            issue(i)
+        each_size(i, lambda c: c.start())
+
+    for i in range(DEPTH - 2):
+        issue(i)
 
     shape = (lam_each, 128)
     row = lax.broadcasted_iota(jnp.int32, shape, 0)
@@ -79,33 +80,27 @@
     moves = old == (me[0] ^ (new // lam_each)) * lam_each + lax.rem(new, lam_each)
     moves = jnp.where(moves, 1.0, 0.0).astype(BF16)
     for b in range(blocks):
-        turned[b] = jnp.dot(occ[b], moves, preferred_element_type=F32).astype(BF16)
-
-    def step(i, carry):
-        b, s = place(i)
-        slot = lax.rem(i, DEPTH)
-
-        @pl.when(i + DEPTH - 1 < total)
-        def _():
-            issue(i + DEPTH - 1)
-
-        c = cost[b, s]
+        whole = jnp.dot(occ[b], moves, preferred_element_type=F32).astype(BF16)
         for k in range(1, units + 1):
-            @pl.when(c == k)
-            def _(k=k):
-                copy(i, k).wait()
-                x = xbuf[slot, :, :, 0:MUC * k].reshape(AUXG * NU, MUC * k)
-                h = jnp.dot(x, turned[b, 0:MUC * k, :], preferred_element_type=F32)
-                ht = h.T.astype(BF16)
-                at = pl.multiple_of((b * slots + s) * lam_each, lam_each)
-                for d in range(dests):
-                    outs[d][pl.ds(at, lam_each), :] = ht[d * lam_each:(d + 1) * lam_each]
+            turned[k - 1, b, 0:MUC * k] = whole[0:MUC * k]
+            if k < units:
+                turned[k - 1, b, MUC * k:] = jnp.zeros_like(whole[MUC * k:])
+
+    def step(t, carry):
+        for i in (2 * t, 2 * t + 1):
+            each_size(i, lambda c: c.wait())
+            issue(i + DEPTH - 2)
+        for i in (2 * t, jnp.minimum(2 * t + 1, total - 1)):
+            b, s = place(i)
+            x = xbuf[lax.rem(i, DEPTH)].reshape(AUXG * NU, MU)
+            h = jnp.dot(x, turned[cost[b, s] - 1, b], preferred_element_type=F32)
+            ht = h.T.astype(BF16)
+            at = pl.multiple_of((b * slots + s) * lam_each, lam_each)
+            for d in range(dests):
+                outs[d][pl.ds(at, lam_each), :] = ht[d * lam_each:(d + 1) * lam_each]
         return carry
 
-    lax.fori_loop(0, total, step, 0)
-
-
-ROWS = NAUX + 32
+    lax.fori_loop(0, (total + 1) // 2, step, 0)
 
 
 def response_kernel(sources, last, *rest):
@@ -120,8 +115,9 @@
     pairs = width // 128
     lam_each = 2 * pairs
     slots = (parts[0].shape[0] - lam_each) // (blocks * lam_each)
-    block_rows = 256
+    block_rows = lhs.shape[0]
     held = block_rows // AUXG
+    reach = z.shape[0] // pairs
 
     for s in range(sources):
         rows = parts[s][blocks * slots * lam_each:, 0:128]
@@ -147,7 +143,7 @@
                         upper = four[i * lam_each:i * lam_each + pairs, cols]
                         lower = four[i * lam_each + pairs:(i + 1) * lam_each, cols]
                         for e, v in enumerate(fold(low, upper, lower)):
-                            z[pl.ds(at * AUXG + 2 * j + e, pairs, stride=ROWS), :] = v
+                            z[pl.ds(at * AUXG + 2 * j + e, pairs, stride=reach), :] = v
                 return carry
 
             lax.fori_loop(0, (n + 3) // 4, spread, 0)
@@ -155,7 +151,7 @@
 
         def multiply(m, carry, b=b, filled=filled):
             for q in range(pairs):
-                start = pl.multiple_of(q * ROWS + m * block_rows, 8)
+                start = pl.multiple_of(q * reach + m * block_rows, 8)
                 lhs[:, q * 128:(q + 1) * 128] = z[pl.ds(start, block_rows), :].astype(BF16)
             acc[...] = lax.dot_general(
                 lhs[...], columns[b], (((1,), (1,)), ((), ())), preferred_element_type=F32,
@@ -203,7 +199,7 @@
         out_specs=[vmem] * dests,
         scratch_shapes=[
             pltpu.VMEM((DEPTH, AUXG, NU, MU), BF16),
-            pltpu.VMEM((blocks, MU, LAM), BF16),
+            pltpu.VMEM((MU // MUC, blocks, MU, LAM), BF16),
             pltpu.SemaphoreType.DMA((DEPTH,)),
         ],
         cost_estimate=pl.CostEstimate(flops=2 * 10**9, bytes_accessed=2 * 10**7, transcendentals=0),
@@ -224,13 +220,16 @@
     running = None
     for number, stage in enumerate(STAGES):
         last = number == len(STAGES) - 1
+        most = len(stage) * slots * AUXG
+        block_rows = min(256, most)
+        reach = -(-most // block_rows) * block_rows + 32
         inputs = [arrived[d] for d in stage]
         specs = [vmem] * len(stage)
         whole = jax.ShapeDtypeStruct((NAUX // 128, NAUX, 128), F32)
         scratch = [
-            pltpu.VMEM((pairs * ROWS, 128), F32),
-            pltpu.VMEM((256, pairs * 128), BF16),
-            pltpu.VMEM((256, NAUX), F32),
+            pltpu.VMEM((pairs * reach, 128), F32),
+            pltpu.VMEM((block_rows, pairs * 128), BF16),
+            pltpu.VMEM((block_rows, NAUX), F32),
             pltpu.VMEM((len(stage), 8, 128), jnp.int32),
             pltpu.SMEM((len(stage), 8, 128), jnp.int32),
             pltpu.SMEM((NGROUPS + 4,), jnp.int32),

time: 130 us -> 124 us (0.954)
  blocking collectives: 41.3 us -> 31.9 us
  starting transfers between devices: 7.76 us -> 15.3 us
  waiting for transfers between devices: 24.1 us -> 20.6 us
    all_to_all x1, blocking collectives: 41.3 us -> 31.9 us  [local(): lax.all_to_all(mine, ('aux', 'chip'), split_axis=0, concat_axis=0, tiled=...]
    ppermute x7, starting transfers between devices: 7.68 us -> 15.2 us  [local(): lax.ppermute(sent[d], 'aux', [(i, i ^ d) for i in range(dests)])]
    ppermute x7, waiting for transfers between devices: 21.5 us -> 18 us  [local(): lax.ppermute(sent[d], 'aux', [(i, i ^ d) for i in range(dests)])]
    pallas_call x1, Pallas kernels: 13.4 us -> 11.9 us  [local(): pl.pallas_call(functools.partial(half_kernel, dests), out_shape=[jax.Shap...]
  transfers between devices with their start and end apart: 8 -> 8, of which waited for: 2 -> 5; matrix products, arithmetic and copies ran while one was open for 20% -> 21% of each run, Pallas kernels for 6% -> 8%
where the time goes in v1:
time: 124 us
  blocking collectives  31.9 us (26%)
  Pallas kernels  26.6 us (21%)
  waiting for transfers between devices  20.6 us (17%)
  starting transfers between devices  15.3 us (12%)
  matrix products  14.7 us (12%)
  local copies, waits for them, and re-layouts  14.1 us (11%)
    all_to_all x1, blocking collectives, local(): lax.all_to_all(mine, ('aux', 'chip'), split_axis=0, concat_axis=0, tiled=...  31.9 us
    ppermute x7, waiting for transfers between devices, local(): lax.ppermute(sent[d], 'aux', [(i, i ^ d) for i in range(dests)])  18 us
    ppermute x7, starting transfers between devices, local(): lax.ppermute(sent[d], 'aux', [(i, i ^ d) for i in range(dests)])  15.2 us
    pallas_call x2, Pallas kernels, local(): running = respond(*inputs, columns)  14.8 us
    dot_general x1, matrix products, local(): jnp.einsum('qbzit,bnt->bqizn', target.reshape(NAUX, blocks, 2, pairs, SIG...  14.7 us
    pallas_call x1, Pallas kernels, local(): pl.pallas_call(functools.partial(half_kernel, dests), out_shape=[jax.Shap...  11.9 us
    reshape x1, local copies, waits for them, and re-layouts, local(): columns = jnp.einsum('qbzit,bnt->bqizn', target.reshape(NAUX, blocks, 2,...  6.25 us
    convert_element_type x1, local copies, waits for them, and re-layouts, local(): columns = jnp.einsum('qbzit,bnt->bqizn', target.reshape(NAUX, blocks, 2,...  4.86 us
  transfers between devices with their start and end apart: 8, of which 5 were waited for; matrix products, arithmetic and copies ran while one was open for 21% of the time, Pallas kernels for 8%

profile of v1, /device:TPU:0, one launch (start us, length us, event | category | flops | bytes accessed | tf_op | source)
XLA Modules:
  0.0 123.9 jit_solution(7546301457473681190)
XLA Ops:
  0.0 0.0 copy-start
  0.0 11.9 %half.1 = (bf16[528,512]{1,0:T(8,128)(2,1)}, bf16[528,512]{1,0:T(8,128)(2,1)}, bf16[528,512]{1,0:T(8,128)(2,1)}, bf16[528,512]{1,0:T(8,128)(2,1)}, bf16[528,512]...) custom-call(s32[2]{0:T(128)} %bitcast.16, s32[2,16]{1,0:T(2,128)} %cost.1, ...), custom_call_target="tpu_custom_call" | custom-call | flops 2000000000 | bytes 20000000 | tf_op jit(solution)/shard_map/half/pallas_call | solution.py:195
  11.9 0.1 collective-permute-start.1
  12.0 0.1 collective-permute-start.2
  12.1 3.4 %collective-permute-start = (bf16[528,512]{1,0:T(8,128)(2,1)}, bf16[528,512]{1,0:T(8,128)(2,1)}, u32[]{:S(2)}, u32[]{:S(2)}) collective-permute-start(bf16[528,512]{1,0:T(8,128)(2,1)} %get-tuple-element.15), channel_id=1, source_target_pairs={{0,112},{16,96},{32,80},{48,64},{64,48},{80,32},{96,16},{112,0},{1... | collective-permute-start | bytes 1622024 | tf_op jit(solution)/shard_map/ppermute | solution.py:213
  15.4 3.1 %collective-permute-start.3 = (bf16[528,512]{1,0:T(8,128)(2,1)}, bf16[528,512]{1,0:T(8,128)(2,1)S(1)}, u32[]{:S(2)}, u32[]{:S(2)}) collective-permute-start(bf16[528,512]{1,0:T(8,128)(2,1)} %get-tuple-element.19), channel_id=1, source_target_pairs={{0,80},{16,64},{32,112},{48,96},{64,16},{80,0},{96,48},{112,32},{1... | collective-permute-start | bytes 1622024 | tf_op jit(solution)/shard_map/ppermute | solution.py:213
  18.5 3.8 %collective-permute-start.4 = (bf16[528,512]{1,0:T(8,128)(2,1)}, bf16[528,512]{1,0:T(8,128)(2,1)S(1)}, u32[]{:S(2)}, u32[]{:S(2)}) collective-permute-start(bf16[528,512]{1,0:T(8,128)(2,1)} %get-tuple-element.20), channel_id=1, source_target_pairs={{0,96},{16,112},{32,64},{48,80},{64,32},{80,48},{96,0},{112,16},{1... | collective-permute-start | bytes 1622024 | tf_op jit(solution)/shard_map/ppermute | solution.py:213
  22.3 6.5 %collective-permute-done.1.rest_1_ = bf16[528,512]{1,0:T(8,128)(2,1)S(1)} collective-permute-done((bf16[528,512]{1,0:T(8,128)(2,1)}, bf16[528,512]{1,0:T(8,128)(2,1)S(1)}, u32[]{:S(2)}, u32[]{:S(2)}) %collective-permute-start.1) | collective-permute-done | bytes 540704 | tf_op jit(solution)/shard_map/ppermute | solution.py:213
  28.8 0.0 collective-permute-start.5
  28.8 0.0 collective-permute-done.2.rest_2_
  28.8 4.8 %collective-permute-start.6 = (bf16[528,512]{1,0:T(8,128)(2,1)}, bf16[528,512]{1,0:T(8,128)(2,1)}, u32[]{:S(2)}, u32[]{:S(2)}) collective-permute-start(bf16[528,512]{1,0:T(8,128)(2,1)} %get-tuple-element.22), channel_id=1, source_target_pairs={{0,64},{16,80},{32,96},{48,112},{64,0},{80,16},{96,32},{112,48},{1... | collective-permute-start | bytes 1622024 | tf_op jit(solution)/shard_map/ppermute | solution.py:213
  33.6 0.0 copy-done
  33.6 14.7 %convert_bitcast_fusion = bf16[2,1024,8,2,64]{1,4,2,3,0:T(8,128)(2,1)} fusion(bf16[1024,2,2,8,128]{4,3,2,1,0:T(8,128)(2,1)} %bitcast.14, bf16[2,64,128]{2,1,0:T(8,128)(2,1)S(1)} %copy-done), kind=kOutput, calls=%fused_computation.2 | convolution fusion | flops 538968064 | bytes 12615680 | tf_op jit(solution)/shard_map/qbzit,bnt->bqizn/dot_general | solution.py:215
  48.3 4.9 %copy.15 = bf16[2,1024,8,2,64]{1,4,3,2,0:T(8,128)(2,1)} copy(bf16[2,1024,8,2,64]{1,4,2,3,0:T(8,128)(2,1)} %convert_bitcast_fusion) | data formatting | bytes 8388608 | tf_op jit(solution)/shard_map/convert_element_type | solution.py:218
  53.1 6.2 %copy.16.rest_7_.rest_3_ = bf16[2,1024,1024]{2,1,0:T(8,128)(2,1)} copy(bf16[2,1024,1024]{1,2,0:T(8,128)(2,1)} %bitcast.13) | data formatting | bytes 8388608 | tf_op jit(solution)/shard_map/reshape | solution.py:218
  59.4 0.0 collective-permute-done.3.rest_3_
  59.4 1.6 %collective-permute-done.4.rest_4_ = bf16[528,512]{1,0:T(8,128)(2,1)S(1)} collective-permute-done((bf16[528,512]{1,0:T(8,128)(2,1)}, bf16[528,512]{1,0:T(8,128)(2,1)S(1)}, u32[]{:S(2)}, u32[]{:S(2)}) %collective-permute-start.4) | collective-permute-done | bytes 540704 | tf_op jit(solution)/shard_map/ppermute | solution.py:213
  61.1 3.1 %collective-permute-done.5.rest_5_ = bf16[528,512]{1,0:T(8,128)(2,1)S(1)} collective-permute-done((bf16[528,512]{1,0:T(8,128)(2,1)}, bf16[528,512]{1,0:T(8,128)(2,1)S(1)}, u32[]{:S(2)}, u32[]{:S(2)}) %collective-permute-start.5) | collective-permute-done | bytes 540704 | tf_op jit(solution)/shard_map/ppermute | solution.py:213
  64.2 6.7 %collective-permute-done.6.rest_6_ = bf16[528,512]{1,0:T(8,128)(2,1)} collective-permute-done((bf16[528,512]{1,0:T(8,128)(2,1)}, bf16[528,512]{1,0:T(8,128)(2,1)}, u32[]{:S(2)}, u32[]{:S(2)}) %collective-permute-start.6) | collective-permute-done | bytes 540704 | tf_op jit(solution)/shard_map/ppermute | solution.py:213
  70.9 0.0 copy-done.3
  70.9 2.2 %copy-done.1 = bf16[2,1024,1024]{2,1,0:T(8,128)(2,1)S(1)} copy-done((bf16[2,1024,1024]{2,1,0:T(8,128)(2,1)S(1)}, bf16[2,1024,1024]{2,1,0:T(8,128)(2,1)}, u32[]{:S(2)}) %copy-start.1) | copy-done | bytes 4194328
  73.1 9.4 %shard_map.73.rest_2_ = f32[8,1024,128]{2,1,0:T(8,128)S(1)} custom-call(bf16[528,512]{1,0:T(8,128)(2,1)S(1)} %copy-done.3, bf16[528,512]{1,0:T(8,128)(2,1)S(1)} %collective-permute-done.1.rest_1_, bf16[528,512]{1,0:T(8,128)(2,1)S(1)} %collective-permute-done.2.rest_2_, bf16[528,512]{1,0:T(8,128)(2,1)S(1)} %collective-permute-done.3.rest_3_, ...), custom_call_target="tpu_custom_call" | custom-call | flops 3000000000 | bytes 10000000 | tf_op jit(solution)/shard_map/pallas_call | solution.py:256
  82.4 0.0 collective-permute-done.rest_1_
  82.4 0.0 copy-done.2
  82.4 5.4 %shard_map.74 = (f32[8,8,64,128]{3,2,1,0:T(8,128)S(1)}, bf16[8,8,64,128]{3,2,1,0:T(8,128)(2,1)S(1)}) custom-call(s32[1]{0:T(128)} %bitcast.rest_0_, bf16[528,512]{1,0:T(8,128)(2,1)} %collective-permute-done.rest_1_, f32[8,1024,128]{2,1,0:T(8,128)S(1)} %shard_map.73.rest_2_, bf16[2,1024,1024]{2,1,0:T(8,128)(2,1)S(1)} %copy-done.2), custom_call_target="tpu_custom_call" | custom-call | flops 3000000000 | bytes 10000000 | tf_op jit(solution)/shard_map/pallas_call | solution.py:256
  87.9 0.1 collective-permute-start.7
  87.9 2.6 %collective-permute-done.7 = bf16[8,8,64,128]{3,2,1,0:T(8,128)(2,1)S(1)} collective-permute-done((bf16[8,8,64,128]{3,2,1,0:T(8,128)(2,1)S(1)}, bf16[8,8,64,128]{3,2,1,0:T(8,128)(2,1)S(1)}, u32[]{:S(2)}, u32[]{:S(2)}) %collective-permute-start.7) | collective-permute-done | bytes 1048608 | tf_op jit(solution)/shard_map/ppermute | solution.py:258
  90.6 0.4 add_convert_fusion
  91.0 31.9 %all_to_all.5 = bf16[64,64,128]{2,1,0:T(8,128)(2,1)S(1)} all-to-all(bf16[64,64,128]{2,1,0:T(8,128)(2,1)S(1)} %bitcast.15), channel_id=1, replica_groups=mesh['aux'=8,'chip'=8,'core'=2] {'aux','chip'}, dimensions={0} | all-to-all | bytes 2097152 | tf_op jit(solution)/shard_map/all_to_all | solution.py:260
  122.9 0.2 convert_reduce_fusion
  123.1 0.1 fusion.5
  123.2 0.7 copy.18
  (4 shorter events, 0.0 us)
Async XLA Ops:
  0.0 33.6 %copy-start = (bf16[2,64,128]{2,1,0:T(8,128)(2,1)S(1)}, bf16[2,64,128]{2,1,0:T(8,128)(2,1)}, u32[]{:S(2)}) copy-start(bf16[2,64,128]{2,1,0:T(8,128)(2,1)} %param.12) | copy-start | bytes 98308
  11.9 16.9 %collective-permute-start.1 = (bf16[528,512]{1,0:T(8,128)(2,1)}, bf16[528,512]{1,0:T(8,128)(2,1)S(1)}, u32[]{:S(2)}, u32[]{:S(2)}) collective-permute-start(bf16[528,512]{1,0:T(8,128)(2,1)} %get-tuple-element.17), channel_id=1, source_target_pairs={{0,16},{16,0},{32,48},{48,32},{64,80},{80,64},{96,112},{112,96},{1... | collective-permute-start | bytes 1622024 | tf_op jit(solution)/shard_map/ppermute | solution.py:213
  12.0 16.9 %collective-permute-start.2 = (bf16[528,512]{1,0:T(8,128)(2,1)}, bf16[528,512]{1,0:T(8,128)(2,1)S(1)}, u32[]{:S(2)}, u32[]{:S(2)}) collective-permute-start(bf16[528,512]{1,0:T(8,128)(2,1)} %get-tuple-element.18), channel_id=1, source_target_pairs={{0,32},{16,48},{32,0},{48,16},{64,96},{80,112},{96,64},{112,80},{1... | collective-permute-start | bytes 1622024 | tf_op jit(solution)/shard_map/ppermute | solution.py:213
  12.1 70.4 %collective-permute-start = (bf16[528,512]{1,0:T(8,128)(2,1)}, bf16[528,512]{1,0:T(8,128)(2,1)}, u32[]{:S(2)}, u32[]{:S(2)}) collective-permute-start(bf16[528,512]{1,0:T(8,128)(2,1)} %get-tuple-element.15), channel_id=1, source_target_pairs={{0,112},{16,96},{32,80},{48,64},{64,48},{80,32},{96,16},{112,0},{1... | collective-permute-start | bytes 1622024 | tf_op jit(solution)/shard_map/ppermute | solution.py:213
  15.4 44.0 %collective-permute-start.3 = (bf16[528,512]{1,0:T(8,128)(2,1)}, bf16[528,512]{1,0:T(8,128)(2,1)S(1)}, u32[]{:S(2)}, u32[]{:S(2)}) collective-permute-start(bf16[528,512]{1,0:T(8,128)(2,1)} %get-tuple-element.19), channel_id=1, source_target_pairs={{0,80},{16,64},{32,112},{48,96},{64,16},{80,0},{96,48},{112,32},{1... | collective-permute-start | bytes 1622024 | tf_op jit(solution)/shard_map/ppermute | solution.py:213
  18.5 42.5 %collective-permute-start.4 = (bf16[528,512]{1,0:T(8,128)(2,1)}, bf16[528,512]{1,0:T(8,128)(2,1)S(1)}, u32[]{:S(2)}, u32[]{:S(2)}) collective-permute-start(bf16[528,512]{1,0:T(8,128)(2,1)} %get-tuple-element.20), channel_id=1, source_target_pairs={{0,96},{16,112},{32,64},{48,80},{64,32},{80,48},{96,0},{112,16},{1... | collective-permute-start | bytes 1622024 | tf_op jit(solution)/shard_map/ppermute | solution.py:213
  28.8 35.3 %collective-permute-start.5 = (bf16[528,512]{1,0:T(8,128)(2,1)}, bf16[528,512]{1,0:T(8,128)(2,1)S(1)}, u32[]{:S(2)}, u32[]{:S(2)}) collective-permute-start(bf16[528,512]{1,0:T(8,128)(2,1)} %get-tuple-element.21), channel_id=1, source_target_pairs={{0,48},{16,32},{32,16},{48,0},{64,112},{80,96},{96,80},{112,64},{1... | collective-permute-start | bytes 1622024 | tf_op jit(solution)/shard_map/ppermute | solution.py:213
  28.8 42.0 %collective-permute-start.6 = (bf16[528,512]{1,0:T(8,128)(2,1)}, bf16[528,512]{1,0:T(8,128)(2,1)}, u32[]{:S(2)}, u32[]{:S(2)}) collective-permute-start(bf16[528,512]{1,0:T(8,128)(2,1)} %get-tuple-element.22), channel_id=1, source_target_pairs={{0,64},{16,80},{32,96},{48,112},{64,0},{80,16},{96,32},{112,48},{1... | collective-permute-start | bytes 1622024 | tf_op jit(solution)/shard_map/ppermute | solution.py:213
  53.1 17.7 %copy-start.3 = (bf16[528,512]{1,0:T(8,128)(2,1)S(1)}, bf16[528,512]{1,0:T(8,128)(2,1)}, u32[]{:S(2)}) copy-start(bf16[528,512]{1,0:T(8,128)(2,1)} %get-tuple-element.16.rest_0_) | copy-start | bytes 1622020
  70.9 2.2 %copy-start.1 = (bf16[2,1024,1024]{2,1,0:T(8,128)(2,1)S(1)}, bf16[2,1024,1024]{2,1,0:T(8,128)(2,1)}, u32[]{:S(2)}) copy-start(bf16[2,1024,1024]{2,1,0:T(8,128)(2,1)} %copy.16.rest_7_.rest_3_) | copy-start | bytes 12582916
  73.1 9.4 %copy-start.2 = (bf16[2,1024,1024]{2,1,0:T(8,128)(2,1)S(1)}, bf16[2,1024,1024]{2,1,0:T(8,128)(2,1)}, u32[]{:S(2)}) copy-start(bf16[2,1024,1024]{2,1,0:T(8,128)(2,1)} %copy.16.rest_7_.rest_3_) | copy-start | bytes 12582916
  87.9 2.7 %collective-permute-start.7 = (bf16[8,8,64,128]{3,2,1,0:T(8,128)(2,1)S(1)}, bf16[8,8,64,128]{3,2,1,0:T(8,128)(2,1)S(1)}, u32[]{:S(2)}, u32[]{:S(2)}) collective-permute-start(bf16[8,8,64,128]{3,2,1,0:T(8,128)(2,1)S(1)} %get-tuple-element.24), channel_id=1, source_target_pairs={{0,1},{1,0},{2,3},{3,2},{4,5},{5,4},{6,7},{7,6},{8,9},{9,8},{10,11... | collective-permute-start | bytes 3145736 | tf_op jit(solution)/shard_map/ppermute | solution.py:258

commit v2 on v1

--- a/solution.py
+++ b/solution.py
@@ -16,10 +16,11 @@
 SIG = 128
 MUC = 128
 NGROUPS = 128
-DEPTH = 6
+UNROLL = 8
+HEAD = 8
 BF16 = jnp.bfloat16
 F32 = jnp.float32
-STAGES = ((0, 1, 2, 5, 6, 3, 4), (7,))
+STAGES = ((0, 2, 6, 1, 5), (3, 7, 4))
 
 
 def fold(low, first, second):
@@ -41,30 +42,32 @@
         b = jnp.where(i < first, 0, 1)
         return b, i - b * first
 
-    def copy(i, k):
+    def each_size(i, act):
         b, s = place(i)
-        slot = lax.rem(i, DEPTH)
+        for k in range(1, units + 1):
+            @pl.when((cost[b, s] == k) & (i < total))
+            def _(k=k):
+                act(b, s, i, k)
+
+    def copy(b, s, i, k):
         return pltpu.make_async_copy(
             x_hbm.at[b, s, :, :, pl.ds(0, MUC * k)],
-            xbuf.at[slot, :, :, pl.ds(0, MUC * k)],
-            sem.at[slot],
+            xbuf.at[i, :, :, pl.ds(0, MUC * k)],
+            sem.at[i],
         )
 
-    def each_size(i, act):
-        b, s = place(i)
-        c = jnp.where(i < DEPTH, units, cost[b, s])
-        for k in range(1, units + 1):
-            @pl.when((c == k) & (i < total))
-            def _(k=k):
-                act(copy(i, k))
-
-    def issue(i):
-        each_size(i, lambda c: c.start())
-
-    for i in range(DEPTH - 2):
-        issue(i)
-
-    shape = (lam_each, 128)
+    def fetch(b, s, i, k):
+        copy(b, s, i, k).start()
+        if k < units:
+            xbuf[i, :, :, MUC * k:] = jnp.zeros((AUXG, NU, MU - MUC * k), BF16)
+
+    def issue(i, carry):
+        each_size(i, fetch)
+        return carry
+
+    lax.fori_loop(0, total, issue, 0)
+
+    shape = (HEAD, 128)
     row = lax.broadcasted_iota(jnp.int32, shape, 0)
     lane = lax.broadcasted_iota(jnp.int32, shape, 1)
     head = jnp.zeros(shape, jnp.int32)
@@ -87,20 +90,23 @@
                 turned[k - 1, b, MUC * k:] = jnp.zeros_like(whole[MUC * k:])
 
     def step(t, carry):
-        for i in (2 * t, 2 * t + 1):
-            each_size(i, lambda c: c.wait())
-            issue(i + DEPTH - 2)
-        for i in (2 * t, jnp.minimum(2 * t + 1, total - 1)):
+        for u in range(UNROLL):
+            each_size(UNROLL * t + u, lambda *which: copy(*which).wait())
+        for u in range(UNROLL):
+            i = jnp.minimum(UNROLL * t + u, total - 1)
             b, s = place(i)
-            x = xbuf[lax.rem(i, DEPTH)].reshape(AUXG * NU, MU)
+            x = xbuf[i].reshape(AUXG * NU, MU)
             h = jnp.dot(x, turned[cost[b, s] - 1, b], preferred_element_type=F32)
-            ht = h.T.astype(BF16)
+            ht = h.astype(BF16).T
             at = pl.multiple_of((b * slots + s) * lam_each, lam_each)
             for d in range(dests):
                 outs[d][pl.ds(at, lam_each), :] = ht[d * lam_each:(d + 1) * lam_each]
         return carry
 
-    lax.fori_loop(0, (total + 1) // 2, step, 0)
+    lax.fori_loop(0, (total + UNROLL - 1) // UNROLL, step, 0)
+
+
+ROWS = NAUX + 32
 
 
 def response_kernel(sources, last, *rest):
@@ -114,14 +120,13 @@
     blocks, _, width = columns.shape
     pairs = width // 128
     lam_each = 2 * pairs
-    slots = (parts[0].shape[0] - lam_each) // (blocks * lam_each)
-    block_rows = lhs.shape[0]
+    slots = (parts[0].shape[0] - HEAD) // (blocks * lam_each)
+    block_rows = 256
     held = block_rows // AUXG
-    reach = z.shape[0] // pairs
 
     for s in range(sources):
         rows = parts[s][blocks * slots * lam_each:, 0:128]
-        headint[s] = rows.astype(F32).astype(jnp.int32)[0:8]
+        headint[s] = rows.astype(F32).astype(jnp.int32)
     to_scalar = pltpu.make_async_copy(headint, table, ssem.at[0])
     to_scalar.start()
     r[...] = before[...] if last else jnp.zeros_like(r)
@@ -143,7 +148,7 @@
                         upper = four[i * lam_each:i * lam_each + pairs, cols]
                         lower = four[i * lam_each + pairs:(i + 1) * lam_each, cols]
                         for e, v in enumerate(fold(low, upper, lower)):
-                            z[pl.ds(at * AUXG + 2 * j + e, pairs, stride=reach), :] = v
+                            z[pl.ds(at * AUXG + 2 * j + e, pairs, stride=ROWS), :] = v
                 return carry
 
             lax.fori_loop(0, (n + 3) // 4, spread, 0)
@@ -151,7 +156,7 @@
 
         def multiply(m, carry, b=b, filled=filled):
             for q in range(pairs):
-                start = pl.multiple_of(q * reach + m * block_rows, 8)
+                start = pl.multiple_of(q * ROWS + m * block_rows, 8)
                 lhs[:, q * 128:(q + 1) * 128] = z[pl.ds(start, block_rows), :].astype(BF16)
             acc[...] = lax.dot_general(
                 lhs[...], columns[b], (((1,), (1,)), ((), ())), preferred_element_type=F32,
@@ -191,16 +196,16 @@
     vmem = pl.BlockSpec(memory_space=pltpu.VMEM)
     hbm = pl.BlockSpec(memory_space=pltpu.MemorySpace.HBM)
 
-    held = (blocks * slots + 1) * lam_each
+    held = blocks * slots * lam_each + HEAD
     sent = pl.pallas_call(
         functools.partial(half_kernel, dests),
         out_shape=[jax.ShapeDtypeStruct((held, AUXG * NU), BF16)] * dests,
         in_specs=[smem, smem, smem, smem, hbm, vmem],
         out_specs=[vmem] * dests,
         scratch_shapes=[
-            pltpu.VMEM((DEPTH, AUXG, NU, MU), BF16),
+            pltpu.VMEM((blocks * slots, AUXG, NU, MU), BF16),
             pltpu.VMEM((MU // MUC, blocks, MU, LAM), BF16),
-            pltpu.SemaphoreType.DMA((DEPTH,)),
+            pltpu.SemaphoreType.DMA((blocks * slots,)),
         ],
         cost_estimate=pl.CostEstimate(flops=2 * 10**9, bytes_accessed=2 * 10**7, transcendentals=0),
         name="half",
@@ -220,16 +225,13 @@
     running = None
     for number, stage in enumerate(STAGES):
         last = number == len(STAGES) - 1
-        most = len(stage) * slots * AUXG
-        block_rows = min(256, most)
-        reach = -(-most // block_rows) * block_rows + 32
         inputs = [arrived[d] for d in stage]
         specs = [vmem] * len(stage)
         whole = jax.ShapeDtypeStruct((NAUX // 128, NAUX, 128), F32)
         scratch = [
-            pltpu.VMEM((pairs * reach, 128), F32),
-            pltpu.VMEM((block_rows, pairs * 128), BF16),
-            pltpu.VMEM((block_rows, NAUX), F32),
+            pltpu.VMEM((pairs * ROWS, 128), F32),
+            pltpu.VMEM((256, pairs * 128), BF16),
+            pltpu.VMEM((256, NAUX), F32),
             pltpu.VMEM((len(stage), 8, 128), jnp.int32),
             pltpu.SMEM((len(stage), 8, 128), jnp.int32),
             pltpu.SMEM((NGROUPS + 4,), jnp.int32),

time: 124 us -> 119 us (0.960)
  starting transfers between devices: 15.3 us -> 10.5 us
  waiting for transfers between devices: 20.6 us -> 22.4 us
  Pallas kernels: 26.6 us -> 24.9 us
    ppermute x7, starting transfers between devices: 15.2 us -> 10.4 us  [local(): lax.ppermute(sent[d], 'aux', [(i, i ^ d) for i in range(dests)])]
    ppermute x7, waiting for transfers between devices: 18 us -> 19.7 us  [local(): lax.ppermute(sent[d], 'aux', [(i, i ^ d) for i in range(dests)])]
  transfers between devices with their start and end apart: 8 -> 8, of which waited for: 5 -> 2; matrix products, arithmetic and copies ran while one was open for 21% -> 22% of each run, Pallas kernels for 8% -> 7%
where the time goes in v2:
time: 119 us
  blocking collectives  31.6 us (27%)
  Pallas kernels  24.9 us (21%)
  waiting for transfers between devices  22.4 us (19%)
  matrix products  14.7 us (12%)
  local copies, waits for them, and re-layouts  14.1 us (12%)
  starting transfers between devices  10.5 us (9%)
    all_to_all x1, blocking collectives, local(): lax.all_to_all(mine, ('aux', 'chip'), split_axis=0, concat_axis=0, tiled=...  31.6 us
    ppermute x7, waiting for transfers between devices, local(): lax.ppermute(sent[d], 'aux', [(i, i ^ d) for i in range(dests)])  19.7 us
    dot_general x1, matrix products, local(): jnp.einsum('qbzit,bnt->bqizn', target.reshape(NAUX, blocks, 2, pairs, SIG...  14.7 us
    pallas_call x2, Pallas kernels, local(): running = respond(*inputs, columns)  13.7 us
    pallas_call x1, Pallas kernels, local(): pl.pallas_call(functools.partial(half_kernel, dests), out_shape=[jax.Shap...  11.2 us
    ppermute x7, starting transfers between devices, local(): lax.ppermute(sent[d], 'aux', [(i, i ^ d) for i in range(dests)])  10.4 us
    reshape x1, local copies, waits for them, and re-layouts, local(): columns = jnp.einsum('qbzit,bnt->bqizn', target.reshape(NAUX, blocks, 2,...  6.25 us
    convert_element_type x1, local copies, waits for them, and re-layouts, local(): columns = jnp.einsum('qbzit,bnt->bqizn', target.reshape(NAUX, blocks, 2,...  4.86 us
  transfers between devices with their start and end apart: 8, of which 2 were waited for; matrix products, arithmetic and copies ran while one was open for 22% of the time, Pallas kernels for 7%

profile of v2, /device:TPU:0, one launch (start us, length us, event | category | flops | bytes accessed | tf_op | source)
XLA Modules:
  0.0 118.8 jit_solution(11463640081853617169)
XLA Ops:
  0.0 0.0 copy-start
  0.0 11.2 %half.1 = (bf16[520,512]{1,0:T(8,128)(2,1)}, bf16[520,512]{1,0:T(8,128)(2,1)}, bf16[520,512]{1,0:T(8,128)(2,1)}, bf16[520,512]{1,0:T(8,128)(2,1)}, bf16[520,512]...) custom-call(s32[2]{0:T(128)} %bitcast.16, s32[2,16]{1,0:T(2,128)} %cost.1, ...), custom_call_target="tpu_custom_call" | custom-call | flops 2000000000 | bytes 20000000 | tf_op jit(solution)/shard_map/half/pallas_call | solution.py:200
  11.2 0.1 collective-permute-start.3
  11.3 0.1 collective-permute-start.4
  11.4 5.3 %collective-permute-start = (bf16[520,512]{1,0:T(8,128)(2,1)}, bf16[520,512]{1,0:T(8,128)(2,1)S(1)}, u32[]{:S(2)}, u32[]{:S(2)}) collective-permute-start(bf16[520,512]{1,0:T(8,128)(2,1)} %get-tuple-element.15), channel_id=1, source_target_pairs={{0,48},{16,32},{32,16},{48,0},{64,112},{80,96},{96,80},{112,64},{1... | collective-permute-start | bytes 1597448 | tf_op jit(solution)/shard_map/ppermute | solution.py:218
  16.7 1.7 %collective-permute-start.1 = (bf16[520,512]{1,0:T(8,128)(2,1)}, bf16[520,512]{1,0:T(8,128)(2,1)S(1)}, u32[]{:S(2)}, u32[]{:S(2)}) collective-permute-start(bf16[520,512]{1,0:T(8,128)(2,1)} %get-tuple-element.16), channel_id=1, source_target_pairs={{0,112},{16,96},{32,80},{48,64},{64,48},{80,32},{96,16},{112,0},{1... | collective-permute-start | bytes 1597448 | tf_op jit(solution)/shard_map/ppermute | solution.py:218
  18.3 0.4 collective-permute-start.2
  18.8 19.7 %collective-permute-done.3.rest_1_ = bf16[520,512]{1,0:T(8,128)(2,1)S(1)} collective-permute-done((bf16[520,512]{1,0:T(8,128)(2,1)}, bf16[520,512]{1,0:T(8,128)(2,1)S(1)}, u32[]{:S(2)}, u32[]{:S(2)}) %collective-permute-start.3) | collective-permute-done | bytes 532512 | tf_op jit(solution)/shard_map/ppermute | solution.py:218
  38.4 0.0 collective-permute-start.5
  38.4 0.0 collective-permute-done.4.rest_2_
  38.5 2.8 %collective-permute-start.6 = (bf16[520,512]{1,0:T(8,128)(2,1)}, bf16[520,512]{1,0:T(8,128)(2,1)}, u32[]{:S(2)}, u32[]{:S(2)}) collective-permute-start(bf16[520,512]{1,0:T(8,128)(2,1)} %get-tuple-element.22), channel_id=1, source_target_pairs={{0,80},{16,64},{32,112},{48,96},{64,16},{80,0},{96,48},{112,32},{1... | collective-permute-start | bytes 1597448 | tf_op jit(solution)/shard_map/ppermute | solution.py:218
  41.3 0.0 copy-done
  41.3 14.7 %convert_bitcast_fusion = bf16[2,1024,8,2,64]{1,4,2,3,0:T(8,128)(2,1)} fusion(bf16[1024,2,2,8,128]{4,3,2,1,0:T(8,128)(2,1)} %bitcast.14, bf16[2,64,128]{2,1,0:T(8,128)(2,1)S(1)} %copy-done), kind=kOutput, calls=%fused_computation.2 | convolution fusion | flops 538968064 | bytes 12615680 | tf_op jit(solution)/shard_map/qbzit,bnt->bqizn/dot_general | solution.py:220
  56.0 4.9 %copy.15 = bf16[2,1024,8,2,64]{1,4,3,2,0:T(8,128)(2,1)} copy(bf16[2,1024,8,2,64]{1,4,2,3,0:T(8,128)(2,1)} %convert_bitcast_fusion) | data formatting | bytes 8388608 | tf_op jit(solution)/shard_map/convert_element_type | solution.py:223
  60.9 6.2 %copy.16.rest_5_ = bf16[2,1024,1024]{2,1,0:T(8,128)(2,1)} copy(bf16[2,1024,1024]{1,2,0:T(8,128)(2,1)} %bitcast.13) | data formatting | bytes 8388608 | tf_op jit(solution)/shard_map/reshape | solution.py:223
  67.1 0.0 collective-permute-done.5.rest_3_
  67.1 0.0 collective-permute-done.6.rest_4_
  67.1 0.0 copy-done.3
  67.1 2.2 %copy-done.1 = bf16[2,1024,1024]{2,1,0:T(8,128)(2,1)S(1)} copy-done((bf16[2,1024,1024]{2,1,0:T(8,128)(2,1)S(1)}, bf16[2,1024,1024]{2,1,0:T(8,128)(2,1)}, u32[]{:S(2)}) %copy-start.1) | copy-done | bytes 4194328
  69.3 8.3 %shard_map.73.rest_4_ = f32[8,1024,128]{2,1,0:T(8,128)S(1)} custom-call(bf16[520,512]{1,0:T(8,128)(2,1)S(1)} %copy-done.3, bf16[520,512]{1,0:T(8,128)(2,1)S(1)} %collective-permute-done.3.rest_1_, bf16[520,512]{1,0:T(8,128)(2,1)S(1)} %collective-permute-done.4.rest_2_, bf16[520,512]{1,0:T(8,128)(2,1)} %collective-permute-done.5.rest_3_, ...), custom_call_target="tpu_custom_call" | custom-call | flops 3000000000 | bytes 10000000 | tf_op jit(solution)/shard_map/pallas_call | solution.py:258
  77.7 0.0 collective-permute-done.rest_1_
  77.7 0.0 collective-permute-done.1.rest_2_
  77.7 0.0 collective-permute-done.2.rest_3_
  77.7 0.0 copy-done.2
  77.7 5.4 %shard_map.74 = (f32[8,8,64,128]{3,2,1,0:T(8,128)S(1)}, bf16[8,8,64,128]{3,2,1,0:T(8,128)(2,1)S(1)}) custom-call(s32[1]{0:T(128)} %bitcast.rest_0_, bf16[520,512]{1,0:T(8,128)(2,1)S(1)} %collective-permute-done.rest_1_, bf16[520,512]{1,0:T(8,128)(2,1)S(1)} %collective-permute-done.1.rest_2_, bf16[520,512]{1,0:T(8,128)(2,1)S(1)} %collective-permute-done.2.rest_3_, ...), custom_call_target="tpu_custom_call" | custom-call | flops 3000000000 | bytes 10000000 | tf_op jit(solution)/shard_map/pallas_call | solution.py:258
  83.1 0.1 collective-permute-start.7
  83.2 2.6 %collective-permute-done.7 = bf16[8,8,64,128]{3,2,1,0:T(8,128)(2,1)S(1)} collective-permute-done((bf16[8,8,64,128]{3,2,1,0:T(8,128)(2,1)S(1)}, bf16[8,8,64,128]{3,2,1,0:T(8,128)(2,1)S(1)}, u32[]{:S(2)}, u32[]{:S(2)}) %collective-permute-start.7) | collective-permute-done | bytes 1048608 | tf_op jit(solution)/shard_map/ppermute | solution.py:260
  85.8 0.4 add_convert_fusion
  86.2 31.6 %all_to_all.5 = bf16[64,64,128]{2,1,0:T(8,128)(2,1)S(1)} all-to-all(bf16[64,64,128]{2,1,0:T(8,128)(2,1)S(1)} %bitcast.15), channel_id=1, replica_groups=mesh['aux'=8,'chip'=8,'core'=2] {'aux','chip'}, dimensions={0} | all-to-all | bytes 2097152 | tf_op jit(solution)/shard_map/all_to_all | solution.py:262
  117.8 0.2 convert_reduce_fusion
  118.0 0.1 fusion.5
  118.1 0.7 copy.18
  (4 shorter events, 0.0 us)
Async XLA Ops:
  0.0 41.3 %copy-start = (bf16[2,64,128]{2,1,0:T(8,128)(2,1)S(1)}, bf16[2,64,128]{2,1,0:T(8,128)(2,1)}, u32[]{:S(2)}) copy-start(bf16[2,64,128]{2,1,0:T(8,128)(2,1)} %param.12) | copy-start | bytes 98308
  11.2 27.2 %collective-permute-start.3 = (bf16[520,512]{1,0:T(8,128)(2,1)}, bf16[520,512]{1,0:T(8,128)(2,1)S(1)}, u32[]{:S(2)}, u32[]{:S(2)}) collective-permute-start(bf16[520,512]{1,0:T(8,128)(2,1)} %get-tuple-element.19), channel_id=1, source_target_pairs={{0,32},{16,48},{32,0},{48,16},{64,96},{80,112},{96,64},{112,80},{1... | collective-permute-start | bytes 1597448 | tf_op jit(solution)/shard_map/ppermute | solution.py:218
  11.3 27.2 %collective-permute-start.4 = (bf16[520,512]{1,0:T(8,128)(2,1)}, bf16[520,512]{1,0:T(8,128)(2,1)S(1)}, u32[]{:S(2)}, u32[]{:S(2)}) collective-permute-start(bf16[520,512]{1,0:T(8,128)(2,1)} %get-tuple-element.20), channel_id=1, source_target_pairs={{0,96},{16,112},{32,64},{48,80},{64,32},{80,48},{96,0},{112,16},{1... | collective-permute-start | bytes 1597448 | tf_op jit(solution)/shard_map/ppermute | solution.py:218
  11.4 66.3 %collective-permute-start = (bf16[520,512]{1,0:T(8,128)(2,1)}, bf16[520,512]{1,0:T(8,128)(2,1)S(1)}, u32[]{:S(2)}, u32[]{:S(2)}) collective-permute-start(bf16[520,512]{1,0:T(8,128)(2,1)} %get-tuple-element.15), channel_id=1, source_target_pairs={{0,48},{16,32},{32,16},{48,0},{64,112},{80,96},{96,80},{112,64},{1... | collective-permute-start | bytes 1597448 | tf_op jit(solution)/shard_map/ppermute | solution.py:218
  16.7 61.0 %collective-permute-start.1 = (bf16[520,512]{1,0:T(8,128)(2,1)}, bf16[520,512]{1,0:T(8,128)(2,1)S(1)}, u32[]{:S(2)}, u32[]{:S(2)}) collective-permute-start(bf16[520,512]{1,0:T(8,128)(2,1)} %get-tuple-element.16), channel_id=1, source_target_pairs={{0,112},{16,96},{32,80},{48,64},{64,48},{80,32},{96,16},{112,0},{1... | collective-permute-start | bytes 1597448 | tf_op jit(solution)/shard_map/ppermute | solution.py:218
  18.3 59.3 %collective-permute-start.2 = (bf16[520,512]{1,0:T(8,128)(2,1)}, bf16[520,512]{1,0:T(8,128)(2,1)S(1)}, u32[]{:S(2)}, u32[]{:S(2)}) collective-permute-start(bf16[520,512]{1,0:T(8,128)(2,1)} %get-tuple-element.17), channel_id=1, source_target_pairs={{0,64},{16,80},{32,96},{48,112},{64,0},{80,16},{96,32},{112,48},{1... | collective-permute-start | bytes 1597448 | tf_op jit(solution)/shard_map/ppermute | solution.py:218
  38.4 28.7 %collective-permute-start.5 = (bf16[520,512]{1,0:T(8,128)(2,1)}, bf16[520,512]{1,0:T(8,128)(2,1)}, u32[]{:S(2)}, u32[]{:S(2)}) collective-permute-start(bf16[520,512]{1,0:T(8,128)(2,1)} %get-tuple-element.21), channel_id=1, source_target_pairs={{0,16},{16,0},{32,48},{48,32},{64,80},{80,64},{96,112},{112,96},{1... | collective-permute-start | bytes 1597448 | tf_op jit(solution)/shard_map/ppermute | solution.py:218
  38.5 28.7 %collective-permute-start.6 = (bf16[520,512]{1,0:T(8,128)(2,1)}, bf16[520,512]{1,0:T(8,128)(2,1)}, u32[]{:S(2)}, u32[]{:S(2)}) collective-permute-start(bf16[520,512]{1,0:T(8,128)(2,1)} %get-tuple-element.22), channel_id=1, source_target_pairs={{0,80},{16,64},{32,112},{48,96},{64,16},{80,0},{96,48},{112,32},{1... | collective-permute-start | bytes 1597448 | tf_op jit(solution)/shard_map/ppermute | solution.py:218
  60.9 6.3 %copy-start.3 = (bf16[520,512]{1,0:T(8,128)(2,1)S(1)}, bf16[520,512]{1,0:T(8,128)(2,1)}, u32[]{:S(2)}) copy-start(bf16[520,512]{1,0:T(8,128)(2,1)} %get-tuple-element.18.rest_0_) | copy-start | bytes 1597444
  67.1 2.2 %copy-start.1 = (bf16[2,1024,1024]{2,1,0:T(8,128)(2,1)S(1)}, bf16[2,1024,1024]{2,1,0:T(8,128)(2,1)}, u32[]{:S(2)}) copy-start(bf16[2,1024,1024]{2,1,0:T(8,128)(2,1)} %copy.16.rest_5_) | copy-start | bytes 12582916
  69.3 8.4 %copy-start.2 = (bf16[2,1024,1024]{2,1,0:T(8,128)(2,1)S(1)}, bf16[2,1024,1024]{2,1,0:T(8,128)(2,1)}, u32[]{:S(2)}) copy-start(bf16[2,1024,1024]{2,1,0:T(8,128)(2,1)} %copy.16.rest_5_) | copy-start | bytes 12582916
  83.1 2.7 %collective-permute-start.7 = (bf16[8,8,64,128]{3,2,1,0:T(8,128)(2,1)S(1)}, bf16[8,8,64,128]{3,2,1,0:T(8,128)(2,1)S(1)}, u32[]{:S(2)}, u32[]{:S(2)}) collective-permute-start(bf16[8,8,64,128]{3,2,1,0:T(8,128)(2,1)S(1)} %get-tuple-element.24), channel_id=1, source_target_pairs={{0,1},{1,0},{2,3},{3,2},{4,5},{5,4},{6,7},{7,6},{8,9},{9,8},{10,11... | collective-permute-start | bytes 3145736 | tf_op jit(solution)/shard_map/ppermute | solution.py:260

commit v3 on v2

--- a/solution.py
+++ b/solution.py
@@ -16,7 +16,7 @@
 SIG = 128
 MUC = 128
 NGROUPS = 128
-UNROLL = 8
+TOGETHER = 4
 HEAD = 8
 BF16 = jnp.bfloat16
 F32 = jnp.float32
@@ -31,41 +31,37 @@
 
 
 def half_kernel(dests, count, cost, group, me, x_hbm, occ, *rest):
-    outs, (xbuf, turned, sem) = rest[:dests], rest[dests:]
+    outs, (xbuf, turned, obuf, headbuf, sem, osem, gsem) = rest[:dests], rest[dests:]
     blocks, slots = cost.shape
     lam_each = LAM // dests
     units = MU // MUC
-    first = count[0]
-    total = first + count[1]
-
-    def place(i):
-        b = jnp.where(i < first, 0, 1)
-        return b, i - b * first
-
-    def each_size(i, act):
-        b, s = place(i)
+    chunks = slots // TOGETHER
+    tall = TOGETHER * lam_each
+
+    def each_size(b, s, act):
         for k in range(1, units + 1):
-            @pl.when((cost[b, s] == k) & (i < total))
+            @pl.when((cost[b, s] == k) & (s < count[b]))
             def _(k=k):
-                act(b, s, i, k)
-
-    def copy(b, s, i, k):
+                act(b, s, k)
+
+    def copy(b, s, k):
         return pltpu.make_async_copy(
             x_hbm.at[b, s, :, :, pl.ds(0, MUC * k)],
-            xbuf.at[i, :, :, pl.ds(0, MUC * k)],
-            sem.at[i],
+            xbuf.at[b * slots + s, :, :, pl.ds(0, MUC * k)],
+            sem.at[b * slots + s],
         )
 
-    def fetch(b, s, i, k):
-        copy(b, s, i, k).start()
+    def fetch(b, s, k):
+        copy(b, s, k).start()
         if k < units:
-            xbuf[i, :, :, MUC * k:] = jnp.zeros((AUXG, NU, MU - MUC * k), BF16)
-
-    def issue(i, carry):
-        each_size(i, fetch)
-        return carry
-
-    lax.fori_loop(0, total, issue, 0)
+            xbuf[b * slots + s, :, :, MUC * k:] = jnp.zeros((AUXG, NU, MU - MUC * k), BF16)
+
+    for b in range(blocks):
+        def issue(s, carry, b=b):
+            each_size(b, s, fetch)
+            return carry
+
+        lax.fori_loop(0, count[b], issue, 0)
 
     shape = (HEAD, 128)
     row = lax.broadcasted_iota(jnp.int32, shape, 0)
@@ -75,48 +71,67 @@
         head = jnp.where((row == b) & (lane == slots), count[b], head)
         for s in range(slots):
             head = jnp.where((row == b) & (lane == s), group[b, s], head)
-    head = head.astype(F32).astype(BF16)
-    for out in outs:
-        out[blocks * slots * lam_each:, 0:128] = head
+    headbuf[...] = head.astype(F32).astype(BF16)
+    end = pl.ds(blocks * slots * lam_each, HEAD)
+    heads = [
+        pltpu.make_async_copy(headbuf, outs[d].at[end, pl.ds(0, 128)], gsem.at[d])
+        for d in range(dests)
+    ]
+    for one in heads:
+        one.start()
     old = lax.broadcasted_iota(jnp.int32, (LAM, LAM), 0)
     new = lax.broadcasted_iota(jnp.int32, (LAM, LAM), 1)
     moves = old == (me[0] ^ (new // lam_each)) * lam_each + lax.rem(new, lam_each)
     moves = jnp.where(moves, 1.0, 0.0).astype(BF16)
     for b in range(blocks):
-        whole = jnp.dot(occ[b], moves, preferred_element_type=F32).astype(BF16)
-        for k in range(1, units + 1):
-            turned[k - 1, b, 0:MUC * k] = whole[0:MUC * k]
-            if k < units:
-                turned[k - 1, b, MUC * k:] = jnp.zeros_like(whole[MUC * k:])
-
-    def step(t, carry):
-        for u in range(UNROLL):
-            each_size(UNROLL * t + u, lambda *which: copy(*which).wait())
-        for u in range(UNROLL):
-            i = jnp.minimum(UNROLL * t + u, total - 1)
-            b, s = place(i)
-            x = xbuf[i].reshape(AUXG * NU, MU)
-            h = jnp.dot(x, turned[cost[b, s] - 1, b], preferred_element_type=F32)
-            ht = h.astype(BF16).T
-            at = pl.multiple_of((b * slots + s) * lam_each, lam_each)
+        turned[b] = jnp.dot(occ[b], moves, preferred_element_type=F32).astype(BF16)
+
+    def out_copy(b, t, d):
+        rows = pl.ds(pl.multiple_of((b * chunks + t) * tall, tall), tall)
+        return pltpu.make_async_copy(
+            obuf.at[d, rows], outs[d].at[rows], osem.at[b * chunks + t, d])
+
+    for b in range(blocks):
+        steps = (count[b] + TOGETHER - 1) // TOGETHER
+
+        def step(t, carry, b=b):
+            for u in range(TOGETHER):
+                each_size(b, TOGETHER * t + u, lambda *which: copy(*which).wait())
+            x = xbuf[pl.ds(b * slots + TOGETHER * t, TOGETHER)].reshape(-1, MU)
+            h = jnp.dot(x, turned[b], preferred_element_type=F32).astype(BF16)
+            for u in range(TOGETHER):
+                ht = h[u * AUXG * NU:(u + 1) * AUXG * NU].T
+                at = pl.multiple_of((b * slots + TOGETHER * t + u) * lam_each, lam_each)
+                for d in range(dests):
+                    obuf[d, pl.ds(at, lam_each), :] = ht[d * lam_each:(d + 1) * lam_each]
             for d in range(dests):
-                outs[d][pl.ds(at, lam_each), :] = ht[d * lam_each:(d + 1) * lam_each]
-        return carry
-
-    lax.fori_loop(0, (total + UNROLL - 1) // UNROLL, step, 0)
+                out_copy(b, t, d).start()
+            return carry
+
+        lax.fori_loop(0, steps, step, 0)
+    for b in range(blocks):
+        def finish(t, carry, b=b):
+            for d in range(dests):
+                out_copy(b, t, d).wait()
+            return carry
+
+        lax.fori_loop(0, (count[b] + TOGETHER - 1) // TOGETHER, finish, 0)
+    for one in heads:
+        one.wait()
 
 
 ROWS = NAUX + 32
 
 
 def response_kernel(sources, last, *rest):
-    if last:
-        core, rest = rest[0], rest[1:]
+    core, rest = rest[0], rest[1:]
+    is_first = core[0] == 0
     parts, rest = rest[:sources], rest[sources:]
     if last:
-        before, columns, keep_ref, send_ref, z, lhs, acc, headint, table, order, ssem, r = rest
+        keep_before, send_before, columns, keep_ref, send_ref = rest[:5]
     else:
-        columns, r, z, lhs, acc, headint, table, order, ssem = rest
+        columns, keep_ref, send_ref = rest[:3]
+    z, lhs, acc, headint, table, order, ssem, r = rest[-8:]
     blocks, _, width = columns.shape
     pairs = width // 128
     lam_each = 2 * pairs
@@ -129,7 +144,11 @@
         headint[s] = rows.astype(F32).astype(jnp.int32)
     to_scalar = pltpu.make_async_copy(headint, table, ssem.at[0])
     to_scalar.start()
-    r[...] = before[...] if last else jnp.zeros_like(r)
+    if last:
+        keep_ref[...] = keep_before[...]
+        r[...] = send_before[...]
+    else:
+        r[...] = jnp.zeros_like(r)
     low = lax.broadcasted_iota(jnp.int32, (8, 128), 1) < 64
     to_scalar.wait()
     for b in range(blocks):
@@ -164,10 +183,21 @@
 
             def scatter(i, inner):
                 g = order[m * held + i]
-                to = pl.ds(pl.multiple_of(g * AUXG, AUXG), AUXG)
                 at = pl.ds(pl.multiple_of(i * AUXG, AUXG), AUXG)
-                for q in range(r.shape[0]):
-                    r[q, to, :] += acc[at, q * 128:(q + 1) * 128]
+                if not last:
+                    to = pl.ds(pl.multiple_of(g * AUXG, AUXG), AUXG)
+                    for q in range(r.shape[0]):
+                        r[q, to, :] += acc[at, q * 128:(q + 1) * 128]
+                    return inner
+                tile, upper = g // 16, lax.rem(g, 16) < 8
+                to = pl.ds(pl.multiple_of(lax.rem(g, 8) * AUXG, AUXG), AUXG)
+                mask = low == upper
+                straight = upper == is_first
+                for q in range(r.shape[1]):
+                    v = acc[at, q * 128:(q + 1) * 128]
+                    w = pltpu.roll(v, 64, 1)
+                    keep_ref[tile, q, to, :] += jnp.where(mask, jnp.where(straight, v, w), 0.0)
+                    r[tile, q, to, :] += jnp.where(mask, jnp.where(straight, w, v), 0.0)
                 return inner
 
             lax.fori_loop(0, jnp.minimum(held, filled - m * held), scatter, 0)
@@ -176,14 +206,14 @@
         lax.fori_loop(0, (filled + held - 1) // held, multiply, 0)
 
     if last:
-        is_first = core[0] == 0
-        low = lax.broadcasted_iota(jnp.int32, (64, 128), 1) < 64
-        for a in range(keep_ref.shape[0]):
-            for q in range(keep_ref.shape[1]):
-                even, odd = fold(
-                    low, r[q, a * 128:a * 128 + 64, :], r[q, a * 128 + 64:a * 128 + 128, :])
-                keep_ref[a, q] = jnp.where(is_first, even, odd)
-                send_ref[a, q] = jnp.where(is_first, odd, even).astype(BF16)
+        send_ref[...] = r[...].astype(BF16)
+        return
+    low = lax.broadcasted_iota(jnp.int32, (64, 128), 1) < 64
+    for a in range(keep_ref.shape[0]):
+        for q in range(keep_ref.shape[1]):
+            even, odd = fold(low, r[q, a * 128:a * 128 + 64, :], r[q, a * 128 + 64:a * 128 + 128, :])
+            keep_ref[a, q] = jnp.where(is_first, even, odd)
+            send_ref[a, q] = jnp.where(is_first, odd, even)
 
 
 def local(three_centre, slot_groups, slot_count, block_cost, green_occ, green_vir, target):
@@ -201,11 +231,15 @@
         functools.partial(half_kernel, dests),
         out_shape=[jax.ShapeDtypeStruct((held, AUXG * NU), BF16)] * dests,
         in_specs=[smem, smem, smem, smem, hbm, vmem],
-        out_specs=[vmem] * dests,
+        out_specs=[hbm] * dests,
         scratch_shapes=[
             pltpu.VMEM((blocks * slots, AUXG, NU, MU), BF16),
-            pltpu.VMEM((MU // MUC, blocks, MU, LAM), BF16),
+            pltpu.VMEM((blocks, MU, LAM), BF16),
+            pltpu.VMEM((dests, blocks * slots * lam_each, AUXG * NU), BF16),
+            pltpu.VMEM((HEAD, 128), BF16),
             pltpu.SemaphoreType.DMA((blocks * slots,)),
+            pltpu.SemaphoreType.DMA((blocks * slots // TOGETHER, dests)),
+            pltpu.SemaphoreType.DMA((dests,)),
         ],
         cost_estimate=pl.CostEstimate(flops=2 * 10**9, bytes_accessed=2 * 10**7, transcendentals=0),
         name="half",
@@ -227,7 +261,6 @@
         last = number == len(STAGES) - 1
         inputs = [arrived[d] for d in stage]
         specs = [vmem] * len(stage)
-        whole = jax.ShapeDtypeStruct((NAUX // 128, NAUX, 128), F32)
         scratch = [
             pltpu.VMEM((pairs * ROWS, 128), F32),
             pltpu.VMEM((256, pairs * 128), BF16),
@@ -237,20 +270,22 @@
             pltpu.SMEM((NGROUPS + 4,), jnp.int32),
             pltpu.SemaphoreType.DMA((1,)),
         ]
-        shape = whole
+        folded = (dests, chips, 64, 128)
+        shape = (
+            jax.ShapeDtypeStruct(folded, F32),
+            jax.ShapeDtypeStruct(folded, BF16 if last else F32),
+        )
+        inputs = [core, *inputs]
+        specs = [smem, *specs]
         if last:
-            inputs = [core, *inputs, running]
-            specs = [smem, *specs, vmem]
-            scratch.append(pltpu.VMEM(whole.shape, F32))
-            shape = (
-                jax.ShapeDtypeStruct((dests, chips, 64, 128), F32),
-                jax.ShapeDtypeStruct((dests, chips, 64, 128), BF16),
-            )
+            inputs += running
+            specs += [vmem, vmem]
+        scratch.append(pltpu.VMEM(folded if last else (NAUX // 128, NAUX, 128), F32))
         respond = pl.pallas_call(
             functools.partial(response_kernel, len(stage), last),
             out_shape=shape,
             in_specs=[*specs, vmem],
-            out_specs=(vmem, vmem) if last else vmem,
+            out_specs=(vmem, vmem),
             scratch_shapes=scratch,
             compiler_params=pltpu.CompilerParams(vmem_limit_bytes=24 * 2**20),
             cost_estimate=pl.CostEstimate(flops=3 * 10**9, bytes_accessed=10**7, transcendentals=0),

time: 119 us -> 122 us (1.025)
  blocking collectives: 31.6 us -> 33.9 us
  Pallas kernels: 24.9 us -> 26.2 us
    pallas_call x2, Pallas kernels: 13.7 us -> 15.9 us  [local(): running = respond(*inputs, columns)]
    all_to_all x1, blocking collectives: 31.6 us -> 33.9 us  [local(): lax.all_to_all(mine, ('aux', 'chip'), split_axis=0, concat_axis=0, tiled=...]
  transfers between devices with their start and end apart: 8 -> 8, of which waited for: 2 -> 2; matrix products, arithmetic and copies ran while one was open for 22% -> 21% of each run, Pallas kernels for 7% -> 8%
where the time goes in v3:
time: 122 us
  blocking collectives  33.9 us (28%)
  Pallas kernels  26.2 us (21%)
  waiting for transfers between devices  22.9 us (19%)
  matrix products  14.7 us (12%)
  local copies, waits for them, and re-layouts  14.1 us (12%)
  starting transfers between devices  9.64 us (8%)
    all_to_all x1, blocking collectives, local(): lax.all_to_all(mine, ('aux', 'chip'), split_axis=0, concat_axis=0, tiled=...  33.9 us
    ppermute x7, waiting for transfers between devices, local(): lax.ppermute(sent[d], 'aux', [(i, i ^ d) for i in range(dests)])  20.2 us
    pallas_call x2, Pallas kernels, local(): running = respond(*inputs, columns)  15.9 us
    dot_general x1, matrix products, local(): jnp.einsum('qbzit,bnt->bqizn', target.reshape(NAUX, blocks, 2, pairs, SIG...  14.7 us
    pallas_call x1, Pallas kernels, local(): pl.pallas_call(functools.partial(half_kernel, dests), out_shape=[jax.Shap...  10.2 us
    ppermute x7, starting transfers between devices, local(): lax.ppermute(sent[d], 'aux', [(i, i ^ d) for i in range(dests)])  9.56 us
    reshape x1, local copies, waits for them, and re-layouts, local(): columns = jnp.einsum('qbzit,bnt->bqizn', target.reshape(NAUX, blocks, 2,...  6.26 us
    convert_element_type x1, local copies, waits for them, and re-layouts, local(): columns = jnp.einsum('qbzit,bnt->bqizn', target.reshape(NAUX, blocks, 2,...  4.87 us
  transfers between devices with their start and end apart: 8, of which 2 were waited for; matrix products, arithmetic and copies ran while one was open for 21% of the time, Pallas kernels for 8%

profile of v3, /device:TPU:0, one launch (start us, length us, event | category | flops | bytes accessed | tf_op | source)
XLA Modules:
  0.0 122.0 jit_solution(3163114471571290061)
XLA Ops:
  0.0 0.0 copy-start
  0.0 10.2 %half.1 = (bf16[520,512]{1,0:T(8,128)(2,1)}, bf16[520,512]{1,0:T(8,128)(2,1)}, bf16[520,512]{1,0:T(8,128)(2,1)}, bf16[520,512]{1,0:T(8,128)(2,1)}, bf16[520,512]...) custom-call(s32[2]{0:T(128)} %bitcast.16, s32[2,16]{1,0:T(2,128)} %cost.1, ...), custom_call_target="tpu_custom_call" | custom-call | flops 2000000000 | bytes 20000000 | tf_op jit(solution)/shard_map/half/pallas_call | solution.py:230
  10.2 0.1 collective-permute-start.3
  10.3 0.2 collective-permute-start.4
  10.6 4.8 %collective-permute-start = (bf16[520,512]{1,0:T(8,128)(2,1)}, bf16[520,512]{1,0:T(8,128)(2,1)S(1)}, u32[]{:S(2)}, u32[]{:S(2)}) collective-permute-start(bf16[520,512]{1,0:T(8,128)(2,1)} %get-tuple-element.17), channel_id=1, source_target_pairs={{0,48},{16,32},{32,16},{48,0},{64,112},{80,96},{96,80},{112,64},{1... | collective-permute-start | bytes 1597448 | tf_op jit(solution)/shard_map/ppermute | solution.py:252
  15.4 2.0 %collective-permute-start.1 = (bf16[520,512]{1,0:T(8,128)(2,1)}, bf16[520,512]{1,0:T(8,128)(2,1)S(1)}, u32[]{:S(2)}, u32[]{:S(2)}) collective-permute-start(bf16[520,512]{1,0:T(8,128)(2,1)} %get-tuple-element.18), channel_id=1, source_target_pairs={{0,112},{16,96},{32,80},{48,64},{64,48},{80,32},{96,16},{112,0},{1... | collective-permute-start | bytes 1597448 | tf_op jit(solution)/shard_map/ppermute | solution.py:252
  17.4 0.1 collective-permute-start.2
  17.4 20.2 %collective-permute-done.3.rest_2_ = bf16[520,512]{1,0:T(8,128)(2,1)S(1)} collective-permute-done((bf16[520,512]{1,0:T(8,128)(2,1)}, bf16[520,512]{1,0:T(8,128)(2,1)S(1)}, u32[]{:S(2)}, u32[]{:S(2)}) %collective-permute-start.3) | collective-permute-done | bytes 532512 | tf_op jit(solution)/shard_map/ppermute | solution.py:252
  37.6 0.0 collective-permute-start.5
  37.6 0.0 collective-permute-done.4.rest_3_
  37.6 2.4 %collective-permute-start.6 = (bf16[520,512]{1,0:T(8,128)(2,1)}, bf16[520,512]{1,0:T(8,128)(2,1)}, u32[]{:S(2)}, u32[]{:S(2)}) collective-permute-start(bf16[520,512]{1,0:T(8,128)(2,1)} %get-tuple-element.24), channel_id=1, source_target_pairs={{0,80},{16,64},{32,112},{48,96},{64,16},{80,0},{96,48},{112,32},{1... | collective-permute-start | bytes 1597448 | tf_op jit(solution)/shard_map/ppermute | solution.py:252
  40.0 0.0 copy-done
  40.0 14.7 %convert_bitcast_fusion = bf16[2,1024,8,2,64]{1,4,2,3,0:T(8,128)(2,1)} fusion(bf16[1024,2,2,8,128]{4,3,2,1,0:T(8,128)(2,1)} %bitcast.14, bf16[2,64,128]{2,1,0:T(8,128)(2,1)S(1)} %copy-done), kind=kOutput, calls=%fused_computation.2 | convolution fusion | flops 538968064 | bytes 12615680 | tf_op jit(solution)/shard_map/qbzit,bnt->bqizn/dot_general | solution.py:254
  54.7 4.9 %copy.15 = bf16[2,1024,8,2,64]{1,4,3,2,0:T(8,128)(2,1)} copy(bf16[2,1024,8,2,64]{1,4,2,3,0:T(8,128)(2,1)} %convert_bitcast_fusion) | data formatting | bytes 8388608 | tf_op jit(solution)/shard_map/convert_element_type | solution.py:257
  59.5 6.3 %copy.16.rest_6_ = bf16[2,1024,1024]{2,1,0:T(8,128)(2,1)} copy(bf16[2,1024,1024]{1,2,0:T(8,128)(2,1)} %bitcast.13) | data formatting | bytes 8388608 | tf_op jit(solution)/shard_map/reshape | solution.py:257
  65.8 0.0 collective-permute-done.5.rest_4_
  65.8 0.0 collective-permute-done.6.rest_5_
  65.8 0.0 copy-done.3
  65.8 0.0 copy-start.1
  65.8 2.2 %copy-done.1 = bf16[2,1024,1024]{2,1,0:T(8,128)(2,1)S(1)} copy-done((bf16[2,1024,1024]{2,1,0:T(8,128)(2,1)S(1)}, bf16[2,1024,1024]{2,1,0:T(8,128)(2,1)}, u32[]{:S(2)}) %copy-start.1) | copy-done | bytes 4194328
  68.0 9.5 %shard_map.73 = (f32[8,8,64,128]{3,2,1,0:T(8,128)S(1)}, f32[8,8,64,128]{3,2,1,0:T(8,128)S(1)}) custom-call(s32[1]{0:T(128)} %bitcast.rest_0_, bf16[520,512]{1,0:T(8,128)(2,1)S(1)} %copy-done.3, bf16[520,512]{1,0:T(8,128)(2,1)S(1)} %collective-permute-done.3.rest_2_, bf16[520,512]{1,0:T(8,128)(2,1)S(1)} %collective-permute-done.4.rest_3_, ...), custom_call_target="tpu_custom_call" | custom-call | flops 3000000000 | bytes 10000000 | tf_op jit(solution)/shard_map/pallas_call | solution.py:293
  77.5 0.0 collective-permute-done.rest_1_
  77.5 0.0 collective-permute-done.1.rest_2_
  77.5 0.0 collective-permute-done.2.rest_3_
  77.5 6.5 %shard_map.74 = (f32[8,8,64,128]{3,2,1,0:T(8,128)S(1)}, bf16[8,8,64,128]{3,2,1,0:T(8,128)(2,1)S(1)}) custom-call(s32[1]{0:T(128)} %bitcast.rest_0_, bf16[520,512]{1,0:T(8,128)(2,1)S(1)} %collective-permute-done.rest_1_, bf16[520,512]{1,0:T(8,128)(2,1)S(1)} %collective-permute-done.1.rest_2_, bf16[520,512]{1,0:T(8,128)(2,1)S(1)} %collective-permute-done.2.rest_3_, ...), custom_call_target="tpu_custom_call" | custom-call | flops 3000000000 | bytes 10000000 | tf_op jit(solution)/shard_map/pallas_call | solution.py:293
  84.0 0.1 collective-permute-start.7
  84.1 2.6 %collective-permute-done.7 = bf16[8,8,64,128]{3,2,1,0:T(8,128)(2,1)S(1)} collective-permute-done((bf16[8,8,64,128]{3,2,1,0:T(8,128)(2,1)S(1)}, bf16[8,8,64,128]{3,2,1,0:T(8,128)(2,1)S(1)}, u32[]{:S(2)}, u32[]{:S(2)}) %collective-permute-start.7) | collective-permute-done | bytes 1048608 | tf_op jit(solution)/shard_map/ppermute | solution.py:295
  86.8 0.4 add_convert_fusion
  87.2 33.9 %all_to_all.5 = bf16[64,64,128]{2,1,0:T(8,128)(2,1)S(1)} all-to-all(bf16[64,64,128]{2,1,0:T(8,128)(2,1)S(1)} %bitcast.15), channel_id=1, replica_groups=mesh['aux'=8,'chip'=8,'core'=2] {'aux','chip'}, dimensions={0} | all-to-all | bytes 2097152 | tf_op jit(solution)/shard_map/all_to_all | solution.py:297
  121.0 0.2 convert_reduce_fusion
  121.2 0.1 fusion.5
  121.3 0.7 copy.18
  (4 shorter events, 0.0 us)
Async XLA Ops:
  0.0 40.0 %copy-start = (bf16[2,64,128]{2,1,0:T(8,128)(2,1)S(1)}, bf16[2,64,128]{2,1,0:T(8,128)(2,1)}, u32[]{:S(2)}) copy-start(bf16[2,64,128]{2,1,0:T(8,128)(2,1)} %param.12) | copy-start | bytes 98308
  10.2 27.4 %collective-permute-start.3 = (bf16[520,512]{1,0:T(8,128)(2,1)}, bf16[520,512]{1,0:T(8,128)(2,1)S(1)}, u32[]{:S(2)}, u32[]{:S(2)}) collective-permute-start(bf16[520,512]{1,0:T(8,128)(2,1)} %get-tuple-element.21), channel_id=1, source_target_pairs={{0,32},{16,48},{32,0},{48,16},{64,96},{80,112},{96,64},{112,80},{1... | collective-permute-start | bytes 1597448 | tf_op jit(solution)/shard_map/ppermute | solution.py:252
  10.3 27.3 %collective-permute-start.4 = (bf16[520,512]{1,0:T(8,128)(2,1)}, bf16[520,512]{1,0:T(8,128)(2,1)S(1)}, u32[]{:S(2)}, u32[]{:S(2)}) collective-permute-start(bf16[520,512]{1,0:T(8,128)(2,1)} %get-tuple-element.22), channel_id=1, source_target_pairs={{0,96},{16,112},{32,64},{48,80},{64,32},{80,48},{96,0},{112,16},{1... | collective-permute-start | bytes 1597448 | tf_op jit(solution)/shard_map/ppermute | solution.py:252
  10.6 67.0 %collective-permute-start = (bf16[520,512]{1,0:T(8,128)(2,1)}, bf16[520,512]{1,0:T(8,128)(2,1)S(1)}, u32[]{:S(2)}, u32[]{:S(2)}) collective-permute-start(bf16[520,512]{1,0:T(8,128)(2,1)} %get-tuple-element.17), channel_id=1, source_target_pairs={{0,48},{16,32},{32,16},{48,0},{64,112},{80,96},{96,80},{112,64},{1... | collective-permute-start | bytes 1597448 | tf_op jit(solution)/shard_map/ppermute | solution.py:252
  15.4 62.2 %collective-permute-start.1 = (bf16[520,512]{1,0:T(8,128)(2,1)}, bf16[520,512]{1,0:T(8,128)(2,1)S(1)}, u32[]{:S(2)}, u32[]{:S(2)}) collective-permute-start(bf16[520,512]{1,0:T(8,128)(2,1)} %get-tuple-element.18), channel_id=1, source_target_pairs={{0,112},{16,96},{32,80},{48,64},{64,48},{80,32},{96,16},{112,0},{1... | collective-permute-start | bytes 1597448 | tf_op jit(solution)/shard_map/ppermute | solution.py:252
  17.4 60.2 %collective-permute-start.2 = (bf16[520,512]{1,0:T(8,128)(2,1)}, bf16[520,512]{1,0:T(8,128)(2,1)S(1)}, u32[]{:S(2)}, u32[]{:S(2)}) collective-permute-start(bf16[520,512]{1,0:T(8,128)(2,1)} %get-tuple-element.19), channel_id=1, source_target_pairs={{0,64},{16,80},{32,96},{48,112},{64,0},{80,16},{96,32},{112,48},{1... | collective-permute-start | bytes 1597448 | tf_op jit(solution)/shard_map/ppermute | solution.py:252
  37.6 28.2 %collective-permute-start.5 = (bf16[520,512]{1,0:T(8,128)(2,1)}, bf16[520,512]{1,0:T(8,128)(2,1)}, u32[]{:S(2)}, u32[]{:S(2)}) collective-permute-start(bf16[520,512]{1,0:T(8,128)(2,1)} %get-tuple-element.23), channel_id=1, source_target_pairs={{0,16},{16,0},{32,48},{48,32},{64,80},{80,64},{96,112},{112,96},{1... | collective-permute-start | bytes 1597448 | tf_op jit(solution)/shard_map/ppermute | solution.py:252
  37.6 28.2 %collective-permute-start.6 = (bf16[520,512]{1,0:T(8,128)(2,1)}, bf16[520,512]{1,0:T(8,128)(2,1)}, u32[]{:S(2)}, u32[]{:S(2)}) collective-permute-start(bf16[520,512]{1,0:T(8,128)(2,1)} %get-tuple-element.24), channel_id=1, source_target_pairs={{0,80},{16,64},{32,112},{48,96},{64,16},{80,0},{96,48},{112,32},{1... | collective-permute-start | bytes 1597448 | tf_op jit(solution)/shard_map/ppermute | solution.py:252
  59.5 6.3 %copy-start.3 = (bf16[520,512]{1,0:T(8,128)(2,1)S(1)}, bf16[520,512]{1,0:T(8,128)(2,1)}, u32[]{:S(2)}) copy-start(bf16[520,512]{1,0:T(8,128)(2,1)} %get-tuple-element.20.rest_1_) | copy-start | bytes 1597444
  65.8 2.2 %copy-start.1 = (bf16[2,1024,1024]{2,1,0:T(8,128)(2,1)S(1)}, bf16[2,1024,1024]{2,1,0:T(8,128)(2,1)}, u32[]{:S(2)}) copy-start(bf16[2,1024,1024]{2,1,0:T(8,128)(2,1)} %copy.16.rest_6_) | copy-start | bytes 12582916
  68.0 9.5 %copy-start.2 = (bf16[2,1024,1024]{2,1,0:T(8,128)(2,1)S(1)}, bf16[2,1024,1024]{2,1,0:T(8,128)(2,1)}, u32[]{:S(2)}) copy-start(bf16[2,1024,1024]{2,1,0:T(8,128)(2,1)} %copy.16.rest_6_) | copy-start | bytes 12582916
  84.0 2.7 %collective-permute-start.7 = (bf16[8,8,64,128]{3,2,1,0:T(8,128)(2,1)S(1)}, bf16[8,8,64,128]{3,2,1,0:T(8,128)(2,1)S(1)}, u32[]{:S(2)}, u32[]{:S(2)}) collective-permute-start(bf16[8,8,64,128]{3,2,1,0:T(8,128)(2,1)S(1)} %get-tuple-element.28), channel_id=1, source_target_pairs={{0,1},{1,0},{2,3},{3,2},{4,5},{5,4},{6,7},{7,6},{8,9},{9,8},{10,11... | collective-permute-start | bytes 3145736 | tf_op jit(solution)/shard_map/ppermute | solution.py:295

commit v4 on v3

--- a/solution.py
+++ b/solution.py
@@ -20,7 +20,7 @@
 HEAD = 8
 BF16 = jnp.bfloat16
 F32 = jnp.float32
-STAGES = ((0, 2, 6, 1, 5), (3, 7, 4))
+STAGES = ((0, 2, 6, 1, 5), (3,), (7, 4))
 
 
 def fold(low, first, second):
@@ -123,15 +123,16 @@
 ROWS = NAUX + 32
 
 
-def response_kernel(sources, last, *rest):
-    core, rest = rest[0], rest[1:]
-    is_first = core[0] == 0
+def response_kernel(sources, begun, last, *rest):
+    if last:
+        core, rest = rest[0], rest[1:]
     parts, rest = rest[:sources], rest[sources:]
     if last:
-        keep_before, send_before, columns, keep_ref, send_ref = rest[:5]
+        before, columns, keep_ref, send_ref, z, lhs, acc, headint, table, order, ssem, r = rest
+    elif begun:
+        before, columns, r, z, lhs, acc, headint, table, order, ssem = rest
     else:
-        columns, keep_ref, send_ref = rest[:3]
-    z, lhs, acc, headint, table, order, ssem, r = rest[-8:]
+        columns, r, z, lhs, acc, headint, table, order, ssem = rest
     blocks, _, width = columns.shape
     pairs = width // 128
     lam_each = 2 * pairs
@@ -144,11 +145,7 @@
         headint[s] = rows.astype(F32).astype(jnp.int32)
     to_scalar = pltpu.make_async_copy(headint, table, ssem.at[0])
     to_scalar.start()
-    if last:
-        keep_ref[...] = keep_before[...]
-        r[...] = send_before[...]
-    else:
-        r[...] = jnp.zeros_like(r)
+    r[...] = before[...] if begun else jnp.zeros_like(r)
     low = lax.broadcasted_iota(jnp.int32, (8, 128), 1) < 64
     to_scalar.wait()
     for b in range(blocks):
@@ -181,39 +178,38 @@
                 lhs[...], columns[b], (((1,), (1,)), ((), ())), preferred_element_type=F32,
             )
 
-            def scatter(i, inner):
-                g = order[m * held + i]
-                at = pl.ds(pl.multiple_of(i * AUXG, AUXG), AUXG)
-                if not last:
+            here = jnp.minimum(held, filled - m * held)
+
+            def scatter(t, inner):
+                places, sums = [], []
+                for u in range(4):
+                    i = t * 4 + u
+                    g = jnp.where(i < here, order[m * held + i], NGROUPS)
                     to = pl.ds(pl.multiple_of(g * AUXG, AUXG), AUXG)
+                    at = pl.ds(pl.multiple_of(i * AUXG, AUXG), AUXG)
+                    places.append(to)
+                    sums.append([
+                        r[q, to, :] + acc[at, q * 128:(q + 1) * 128] for q in range(r.shape[0])
+                    ])
+                for to, sum_here in zip(places, sums):
                     for q in range(r.shape[0]):
-                        r[q, to, :] += acc[at, q * 128:(q + 1) * 128]
-                    return inner
-                tile, upper = g // 16, lax.rem(g, 16) < 8
-                to = pl.ds(pl.multiple_of(lax.rem(g, 8) * AUXG, AUXG), AUXG)
-                mask = low == upper
-                straight = upper == is_first
-                for q in range(r.shape[1]):
-                    v = acc[at, q * 128:(q + 1) * 128]
-                    w = pltpu.roll(v, 64, 1)
-                    keep_ref[tile, q, to, :] += jnp.where(mask, jnp.where(straight, v, w), 0.0)
-                    r[tile, q, to, :] += jnp.where(mask, jnp.where(straight, w, v), 0.0)
+                        r[q, to, :] = sum_here[q]
                 return inner
 
-            lax.fori_loop(0, jnp.minimum(held, filled - m * held), scatter, 0)
+            lax.fori_loop(0, (here + 3) // 4, scatter, 0)
             return carry
 
         lax.fori_loop(0, (filled + held - 1) // held, multiply, 0)
 
     if last:
-        send_ref[...] = r[...].astype(BF16)
-        return
-    low = lax.broadcasted_iota(jnp.int32, (64, 128), 1) < 64
-    for a in range(keep_ref.shape[0]):
-        for q in range(keep_ref.shape[1]):
-            even, odd = fold(low, r[q, a * 128:a * 128 + 64, :], r[q, a * 128 + 64:a * 128 + 128, :])
-            keep_ref[a, q] = jnp.where(is_first, even, odd)
-            send_ref[a, q] = jnp.where(is_first, odd, even)
+        is_first = core[0] == 0
+        low = lax.broadcasted_iota(jnp.int32, (64, 128), 1) < 64
+        for a in range(keep_ref.shape[0]):
+            for q in range(keep_ref.shape[1]):
+                even, odd = fold(
+                    low, r[q, a * 128:a * 128 + 64, :], r[q, a * 128 + 64:a * 128 + 128, :])
+                keep_ref[a, q] = jnp.where(is_first, even, odd)
+                send_ref[a, q] = jnp.where(is_first, odd, even).astype(BF16)
 
 
 def local(three_centre, slot_groups, slot_count, block_cost, green_occ, green_vir, target):
@@ -261,6 +257,7 @@
         last = number == len(STAGES) - 1
         inputs = [arrived[d] for d in stage]
         specs = [vmem] * len(stage)
+        whole = jax.ShapeDtypeStruct((NAUX // 128, NAUX + AUXG, 128), F32)
         scratch = [
             pltpu.VMEM((pairs * ROWS, 128), F32),
             pltpu.VMEM((256, pairs * 128), BF16),
@@ -270,22 +267,23 @@
             pltpu.SMEM((NGROUPS + 4,), jnp.int32),
             pltpu.SemaphoreType.DMA((1,)),
         ]
-        folded = (dests, chips, 64, 128)
-        shape = (
-            jax.ShapeDtypeStruct(folded, F32),
-            jax.ShapeDtypeStruct(folded, BF16 if last else F32),
-        )
-        inputs = [core, *inputs]
-        specs = [smem, *specs]
+        shape = whole
+        if number:
+            inputs.append(running)
+            specs.append(vmem)
         if last:
-            inputs += running
-            specs += [vmem, vmem]
-        scratch.append(pltpu.VMEM(folded if last else (NAUX // 128, NAUX, 128), F32))
+            inputs = [core, *inputs]
+            specs = [smem, *specs]
+            scratch.append(pltpu.VMEM(whole.shape, F32))
+            shape = (
+                jax.ShapeDtypeStruct((dests, chips, 64, 128), F32),
+                jax.ShapeDtypeStruct((dests, chips, 64, 128), BF16),
+            )
         respond = pl.pallas_call(
-            functools.partial(response_kernel, len(stage), last),
+            functools.partial(response_kernel, len(stage), number > 0, last),
             out_shape=shape,
             in_specs=[*specs, vmem],
-            out_specs=(vmem, vmem),
+            out_specs=(vmem, vmem) if last else vmem,
             scratch_shapes=scratch,
             compiler_params=pltpu.CompilerParams(vmem_limit_bytes=24 * 2**20),
             cost_estimate=pl.CostEstimate(flops=3 * 10**9, bytes_accessed=10**7, transcendentals=0),

time: 122 us -> 110 us (0.902)
  waiting for transfers between devices: 22.9 us -> 13.6 us
  blocking collectives: 33.9 us -> 28.7 us
  starting transfers between devices: 9.64 us -> 13.7 us
  Pallas kernels: 26.2 us -> 24.4 us
    ppermute x7, waiting for transfers between devices: 20.2 us -> 11 us  [local(): lax.ppermute(sent[d], 'aux', [(i, i ^ d) for i in range(dests)])]
    all_to_all x1, blocking collectives: 33.9 us -> 28.7 us  [local(): lax.all_to_all(mine, ('aux', 'chip'), split_axis=0, concat_axis=0, tiled=...]
    ppermute x7, starting transfers between devices: 9.56 us -> 13.6 us  [local(): lax.ppermute(sent[d], 'aux', [(i, i ^ d) for i in range(dests)])]
    pallas_call x2 -> x3, Pallas kernels: 15.9 us -> 14.1 us  [local(): running = respond(*inputs, columns)]
  transfers between devices with their start and end apart: 8 -> 8, of which waited for: 2 -> 3; matrix products, arithmetic and copies ran while one was open for 21% -> 23% of each run, Pallas kernels for 8% -> 9%
where the time goes in v4:
time: 110 us
  blocking collectives  28.7 us (26%)
  Pallas kernels  24.4 us (22%)
  matrix products  14.7 us (13%)
  local copies, waits for them, and re-layouts  14.1 us (13%)
  starting transfers between devices  13.7 us (12%)
  waiting for transfers between devices  13.6 us (12%)
    all_to_all x1, blocking collectives, local(): lax.all_to_all(mine, ('aux', 'chip'), split_axis=0, concat_axis=0, tiled=...  28.7 us
    dot_general x1, matrix products, local(): jnp.einsum('qbzit,bnt->bqizn', target.reshape(NAUX, blocks, 2, pairs, SIG...  14.7 us
    pallas_call x3, Pallas kernels, local(): running = respond(*inputs, columns)  14.1 us
    ppermute x7, starting transfers between devices, local(): lax.ppermute(sent[d], 'aux', [(i, i ^ d) for i in range(dests)])  13.6 us
    ppermute x7, waiting for transfers between devices, local(): lax.ppermute(sent[d], 'aux', [(i, i ^ d) for i in range(dests)])  11 us
    pallas_call x1, Pallas kernels, local(): pl.pallas_call(functools.partial(half_kernel, dests), out_shape=[jax.Shap...  10.2 us
    reshape x1, local copies, waits for them, and re-layouts, local(): columns = jnp.einsum('qbzit,bnt->bqizn', target.reshape(NAUX, blocks, 2,...  6.25 us
    convert_element_type x1, local copies, waits for them, and re-layouts, local(): columns = jnp.einsum('qbzit,bnt->bqizn', target.reshape(NAUX, blocks, 2,...  4.86 us
  transfers between devices with their start and end apart: 8, of which 3 were waited for; matrix products, arithmetic and copies ran while one was open for 23% of the time, Pallas kernels for 9%

profile of v4, /device:TPU:0, one launch (start us, length us, event | category | flops | bytes accessed | tf_op | source)
XLA Modules:
  0.0 109.8 jit_solution(1292984600600632606)
XLA Ops:
  0.0 0.0 copy-start
  0.0 10.2 %half.1 = (bf16[520,512]{1,0:T(8,128)(2,1)}, bf16[520,512]{1,0:T(8,128)(2,1)}, bf16[520,512]{1,0:T(8,128)(2,1)}, bf16[520,512]{1,0:T(8,128)(2,1)}, bf16[520,512]...) custom-call(s32[2]{0:T(128)} %bitcast.16, s32[2,16]{1,0:T(2,128)} %cost.1, ...), custom_call_target="tpu_custom_call" | custom-call | flops 2000000000 | bytes 20000000 | tf_op jit(solution)/shard_map/half/pallas_call | solution.py:226
  10.3 0.3 collective-permute-start.2
  10.6 0.0 collective-permute-start.3
  10.6 5.4 %collective-permute-start.4 = (bf16[520,512]{1,0:T(8,128)(2,1)}, bf16[520,512]{1,0:T(8,128)(2,1)S(1)}, u32[]{:S(2)}, u32[]{:S(2)}) collective-permute-start(bf16[520,512]{1,0:T(8,128)(2,1)} %get-tuple-element.20), channel_id=1, source_target_pairs={{0,96},{16,112},{32,64},{48,80},{64,32},{80,48},{96,0},{112,16},{1... | collective-permute-start | bytes 1597448 | tf_op jit(solution)/shard_map/ppermute | solution.py:248
  16.0 0.0 collective-permute-start.5
  16.0 2.4 %collective-permute-start.6 = (bf16[520,512]{1,0:T(8,128)(2,1)}, bf16[520,512]{1,0:T(8,128)(2,1)S(1)}, u32[]{:S(2)}, u32[]{:S(2)}) collective-permute-start(bf16[520,512]{1,0:T(8,128)(2,1)} %get-tuple-element.22), channel_id=1, source_target_pairs={{0,80},{16,64},{32,112},{48,96},{64,16},{80,0},{96,48},{112,32},{1... | collective-permute-start | bytes 1597448 | tf_op jit(solution)/shard_map/ppermute | solution.py:248
  18.4 0.0 copy-done
  18.4 14.7 %convert_bitcast_fusion = bf16[2,1024,8,2,64]{1,4,2,3,0:T(8,128)(2,1)} fusion(bf16[1024,2,2,8,128]{4,3,2,1,0:T(8,128)(2,1)} %bitcast.14, bf16[2,64,128]{2,1,0:T(8,128)(2,1)S(1)} %copy-done), kind=kOutput, calls=%fused_computation.2 | convolution fusion | flops 538968064 | bytes 12615680 | tf_op jit(solution)/shard_map/qbzit,bnt->bqizn/dot_general | solution.py:250
  33.1 4.9 %copy.16 = bf16[2,1024,8,2,64]{1,4,3,2,0:T(8,128)(2,1)} copy(bf16[2,1024,8,2,64]{1,4,2,3,0:T(8,128)(2,1)} %convert_bitcast_fusion) | data formatting | bytes 8388608 | tf_op jit(solution)/shard_map/convert_element_type | solution.py:253
  37.9 6.2 %copy.17.rest_5_.rest_2_.rest_4_ = bf16[2,1024,1024]{2,1,0:T(8,128)(2,1)} copy(bf16[2,1024,1024]{1,2,0:T(8,128)(2,1)} %bitcast.13) | data formatting | bytes 8388608 | tf_op jit(solution)/shard_map/reshape | solution.py:253
  44.2 0.0 collective-permute-done.3.rest_1_
  44.2 2.7 %collective-permute-start = (bf16[520,512]{1,0:T(8,128)(2,1)}, bf16[520,512]{1,0:T(8,128)(2,1)S(1)}, u32[]{:S(2)}, u32[]{:S(2)}) collective-permute-start(bf16[520,512]{1,0:T(8,128)(2,1)} %get-tuple-element.15), channel_id=1, source_target_pairs={{0,112},{16,96},{32,80},{48,64},{64,48},{80,32},{96,16},{112,0},{1... | collective-permute-start | bytes 1597448 | tf_op jit(solution)/shard_map/ppermute | solution.py:248
  46.9 0.0 collective-permute-done.4.rest_2_
  46.9 2.8 %collective-permute-start.1 = (bf16[520,512]{1,0:T(8,128)(2,1)}, bf16[520,512]{1,0:T(8,128)(2,1)S(1)}, u32[]{:S(2)}, u32[]{:S(2)}) collective-permute-start(bf16[520,512]{1,0:T(8,128)(2,1)} %get-tuple-element.16), channel_id=1, source_target_pairs={{0,64},{16,80},{32,96},{48,112},{64,0},{80,16},{96,32},{112,48},{1... | collective-permute-start | bytes 1597448 | tf_op jit(solution)/shard_map/ppermute | solution.py:248
  49.7 0.0 collective-permute-done.5.rest_3_
  49.7 0.0 collective-permute-done.6.rest_4_
  49.7 0.0 copy-done.3
  49.7 2.2 %copy-done.1 = bf16[2,1024,1024]{2,1,0:T(8,128)(2,1)S(1)} copy-done((bf16[2,1024,1024]{2,1,0:T(8,128)(2,1)S(1)}, bf16[2,1024,1024]{2,1,0:T(8,128)(2,1)}, u32[]{:S(2)}) %copy-start.1) | copy-done | bytes 4194328
  51.9 6.8 %shard_map.73.rest_1_ = f32[8,1032,128]{2,1,0:T(8,128)S(1)} custom-call(bf16[520,512]{1,0:T(8,128)(2,1)S(1)} %copy-done.3, bf16[520,512]{1,0:T(8,128)(2,1)S(1)} %collective-permute-done.3.rest_1_, bf16[520,512]{1,0:T(8,128)(2,1)S(1)} %collective-permute-done.4.rest_2_, bf16[520,512]{1,0:T(8,128)(2,1)S(1)} %collective-permute-done.5.rest_3_, ...), custom_call_target="tpu_custom_call" | custom-call | flops 3000000000 | bytes 10000000 | tf_op jit(solution)/shard_map/pallas_call | solution.py:291
  58.7 0.0 collective-permute-done.2.rest_0_
  58.7 2.7 %shard_map.74.rest_3_ = f32[8,1032,128]{2,1,0:T(8,128)S(1)} custom-call(bf16[520,512]{1,0:T(8,128)(2,1)S(1)} %collective-permute-done.2.rest_0_, f32[8,1032,128]{2,1,0:T(8,128)S(1)} %shard_map.73.rest_1_, bf16[2,1024,1024]{2,1,0:T(8,128)(2,1)S(1)} %copy-done.2), custom_call_target="tpu_custom_call" | custom-call | flops 3000000000 | bytes 10000000 | tf_op jit(solution)/shard_map/pallas_call | solution.py:291
  61.4 6.4 %collective-permute-done.rest_1_ = bf16[520,512]{1,0:T(8,128)(2,1)S(1)} collective-permute-done((bf16[520,512]{1,0:T(8,128)(2,1)}, bf16[520,512]{1,0:T(8,128)(2,1)S(1)}, u32[]{:S(2)}, u32[]{:S(2)}) %collective-permute-start) | collective-permute-done | bytes 532512 | tf_op jit(solution)/shard_map/ppermute | solution.py:248
  67.8 4.6 %collective-permute-done.1.rest_2_ = bf16[520,512]{1,0:T(8,128)(2,1)S(1)} collective-permute-done((bf16[520,512]{1,0:T(8,128)(2,1)}, bf16[520,512]{1,0:T(8,128)(2,1)S(1)}, u32[]{:S(2)}, u32[]{:S(2)}) %collective-permute-start.1) | collective-permute-done | bytes 532512 | tf_op jit(solution)/shard_map/ppermute | solution.py:248
  72.4 4.7 %shard_map.75 = (f32[8,8,64,128]{3,2,1,0:T(8,128)S(1)}, bf16[8,8,64,128]{3,2,1,0:T(8,128)(2,1)S(1)}) custom-call(s32[1]{0:T(128)} %bitcast.rest_0_, bf16[520,512]{1,0:T(8,128)(2,1)S(1)} %collective-permute-done.rest_1_, bf16[520,512]{1,0:T(8,128)(2,1)S(1)} %collective-permute-done.1.rest_2_, f32[8,1032,128]{2,1,0:T(8,128)S(1)} %shard_map.74.rest_3_, ...), custom_call_target="tpu_custom_call" | custom-call | flops 3000000000 | bytes 10000000 | tf_op jit(solution)/shard_map/pallas_call | solution.py:291
  77.1 0.1 collective-permute-start.7
  77.2 2.6 %collective-permute-done.7 = bf16[8,8,64,128]{3,2,1,0:T(8,128)(2,1)S(1)} collective-permute-done((bf16[8,8,64,128]{3,2,1,0:T(8,128)(2,1)S(1)}, bf16[8,8,64,128]{3,2,1,0:T(8,128)(2,1)S(1)}, u32[]{:S(2)}, u32[]{:S(2)}) %collective-permute-start.7) | collective-permute-done | bytes 1048608 | tf_op jit(solution)/shard_map/ppermute | solution.py:293
  79.8 0.3 add_convert_fusion
  80.2 28.7 %all_to_all.5 = bf16[64,64,128]{2,1,0:T(8,128)(2,1)S(1)} all-to-all(bf16[64,64,128]{2,1,0:T(8,128)(2,1)S(1)} %bitcast.15), channel_id=1, replica_groups=mesh['aux'=8,'chip'=8,'core'=2] {'aux','chip'}, dimensions={0} | all-to-all | bytes 2097152 | tf_op jit(solution)/shard_map/all_to_all | solution.py:295
  108.8 0.2 convert_reduce_fusion
  109.0 0.1 fusion.5
  109.1 0.7 copy.20
  (5 shorter events, 0.0 us)
Async XLA Ops:
  0.0 18.4 %copy-start = (bf16[2,64,128]{2,1,0:T(8,128)(2,1)S(1)}, bf16[2,64,128]{2,1,0:T(8,128)(2,1)}, u32[]{:S(2)}) copy-start(bf16[2,64,128]{2,1,0:T(8,128)(2,1)} %param.12) | copy-start | bytes 98308
  10.3 48.5 %collective-permute-start.2 = (bf16[520,512]{1,0:T(8,128)(2,1)}, bf16[520,512]{1,0:T(8,128)(2,1)S(1)}, u32[]{:S(2)}, u32[]{:S(2)}) collective-permute-start(bf16[520,512]{1,0:T(8,128)(2,1)} %get-tuple-element.17), channel_id=1, source_target_pairs={{0,48},{16,32},{32,16},{48,0},{64,112},{80,96},{96,80},{112,64},{1... | collective-permute-start | bytes 1597448 | tf_op jit(solution)/shard_map/ppermute | solution.py:248
  10.6 33.6 %collective-permute-start.3 = (bf16[520,512]{1,0:T(8,128)(2,1)}, bf16[520,512]{1,0:T(8,128)(2,1)S(1)}, u32[]{:S(2)}, u32[]{:S(2)}) collective-permute-start(bf16[520,512]{1,0:T(8,128)(2,1)} %get-tuple-element.19), channel_id=1, source_target_pairs={{0,32},{16,48},{32,0},{48,16},{64,96},{80,112},{96,64},{112,80},{1... | collective-permute-start | bytes 1597448 | tf_op jit(solution)/shard_map/ppermute | solution.py:248
  10.6 36.4 %collective-permute-start.4 = (bf16[520,512]{1,0:T(8,128)(2,1)}, bf16[520,512]{1,0:T(8,128)(2,1)S(1)}, u32[]{:S(2)}, u32[]{:S(2)}) collective-permute-start(bf16[520,512]{1,0:T(8,128)(2,1)} %get-tuple-element.20), channel_id=1, source_target_pairs={{0,96},{16,112},{32,64},{48,80},{64,32},{80,48},{96,0},{112,16},{1... | collective-permute-start | bytes 1597448 | tf_op jit(solution)/shard_map/ppermute | solution.py:248
  16.0 33.7 %collective-permute-start.5 = (bf16[520,512]{1,0:T(8,128)(2,1)}, bf16[520,512]{1,0:T(8,128)(2,1)S(1)}, u32[]{:S(2)}, u32[]{:S(2)}) collective-permute-start(bf16[520,512]{1,0:T(8,128)(2,1)} %get-tuple-element.21), channel_id=1, source_target_pairs={{0,16},{16,0},{32,48},{48,32},{64,80},{80,64},{96,112},{112,96},{1... | collective-permute-start | bytes 1597448 | tf_op jit(solution)/shard_map/ppermute | solution.py:248
  16.0 33.7 %collective-permute-start.6 = (bf16[520,512]{1,0:T(8,128)(2,1)}, bf16[520,512]{1,0:T(8,128)(2,1)S(1)}, u32[]{:S(2)}, u32[]{:S(2)}) collective-permute-start(bf16[520,512]{1,0:T(8,128)(2,1)} %get-tuple-element.22), channel_id=1, source_target_pairs={{0,80},{16,64},{32,112},{48,96},{64,16},{80,0},{96,48},{112,32},{1... | collective-permute-start | bytes 1597448 | tf_op jit(solution)/shard_map/ppermute | solution.py:248
  37.9 11.8 %copy-start.3 = (bf16[520,512]{1,0:T(8,128)(2,1)S(1)}, bf16[520,512]{1,0:T(8,128)(2,1)}, u32[]{:S(2)}) copy-start(bf16[520,512]{1,0:T(8,128)(2,1)} %get-tuple-element.18.rest_0_) | copy-start | bytes 1597444
  44.2 23.6 %collective-permute-start = (bf16[520,512]{1,0:T(8,128)(2,1)}, bf16[520,512]{1,0:T(8,128)(2,1)S(1)}, u32[]{:S(2)}, u32[]{:S(2)}) collective-permute-start(bf16[520,512]{1,0:T(8,128)(2,1)} %get-tuple-element.15), channel_id=1, source_target_pairs={{0,112},{16,96},{32,80},{48,64},{64,48},{80,32},{96,16},{112,0},{1... | collective-permute-start | bytes 1597448 | tf_op jit(solution)/shard_map/ppermute | solution.py:248
  46.9 25.5 %collective-permute-start.1 = (bf16[520,512]{1,0:T(8,128)(2,1)}, bf16[520,512]{1,0:T(8,128)(2,1)S(1)}, u32[]{:S(2)}, u32[]{:S(2)}) collective-permute-start(bf16[520,512]{1,0:T(8,128)(2,1)} %get-tuple-element.16), channel_id=1, source_target_pairs={{0,64},{16,80},{32,96},{48,112},{64,0},{80,16},{96,32},{112,48},{1... | collective-permute-start | bytes 1597448 | tf_op jit(solution)/shard_map/ppermute | solution.py:248
  49.7 2.2 %copy-start.1 = (bf16[2,1024,1024]{2,1,0:T(8,128)(2,1)S(1)}, bf16[2,1024,1024]{2,1,0:T(8,128)(2,1)}, u32[]{:S(2)}) copy-start(bf16[2,1024,1024]{2,1,0:T(8,128)(2,1)} %copy.17.rest_5_.rest_2_.rest_4_) | copy-start | bytes 12582916
  51.9 6.8 %copy-start.2 = (bf16[2,1024,1024]{2,1,0:T(8,128)(2,1)S(1)}, bf16[2,1024,1024]{2,1,0:T(8,128)(2,1)}, u32[]{:S(2)}) copy-start(bf16[2,1024,1024]{2,1,0:T(8,128)(2,1)} %copy.17.rest_5_.rest_2_.rest_4_) | copy-start | bytes 12582916
  77.1 2.7 %collective-permute-start.7 = (bf16[8,8,64,128]{3,2,1,0:T(8,128)(2,1)S(1)}, bf16[8,8,64,128]{3,2,1,0:T(8,128)(2,1)S(1)}, u32[]{:S(2)}, u32[]{:S(2)}) collective-permute-start(bf16[8,8,64,128]{3,2,1,0:T(8,128)(2,1)S(1)} %get-tuple-element.24), channel_id=1, source_target_pairs={{0,1},{1,0},{2,3},{3,2},{4,5},{5,4},{6,7},{7,6},{8,9},{9,8},{10,11... | collective-permute-start | bytes 3145736 | tf_op jit(solution)/shard_map/ppermute | solution.py:293

commit v5 on v4

--- a/solution.py
+++ b/solution.py
@@ -20,7 +20,8 @@
 HEAD = 8
 BF16 = jnp.bfloat16
 F32 = jnp.float32
-STAGES = ((0, 2, 6, 1, 5), (3,), (7, 4))
+STAGES = ((0, 2, 6, 4), (5, 3), (1, 7))
+ISSUE = (5, 2, 3, 6, 7, 4, 1)
 
 
 def fold(low, first, second):
@@ -241,11 +242,16 @@
         name="half",
     )(slot_count.reshape(-1), block_cost, slot_groups, lax.axis_index("aux").reshape(1),
       three_centre, green_occ)
+
+    def swap(value, d):
+        return lax.ppermute(value, "aux", [(i, i ^ d) for i in range(dests)])
+
     arrived = {0: sent[0]}
-    for stage in STAGES:
-        for d in stage:
-            if d:
-                arrived[d] = lax.ppermute(sent[d], "aux", [(i, i ^ d) for i in range(dests)])
+    for d in ISSUE:
+        arrived[d] = swap(sent[d], 1 if d % 2 else d)
+    for d in ISSUE:
+        if d % 2 and d > 1:
+            arrived[d] = swap(arrived[d], d - 1)
 
     columns = jnp.einsum(
         "qbzit,bnt->bqizn", target.reshape(NAUX, blocks, 2, pairs, SIG), green_vir,

time: 110 us -> 129 us (1.17)
  waiting for transfers between devices: 13.6 us -> 31.6 us
    ppermute x7 -> x10, waiting for transfers between devices: 11 us -> 28.9 us  [swap(): return lax.ppermute(value, 'aux', [(i, i ^ d) for i in range(dests)])]
    unnamed x8 -> x10, local copies, waits for them, and re-layouts: 2.19 us -> 3 us
    ppermute x7 -> x10, starting transfers between devices: 13.6 us -> 14 us  [swap(): return lax.ppermute(value, 'aux', [(i, i ^ d) for i in range(dests)])]
  transfers between devices with their start and end apart: 8 -> 11, of which waited for: 3 -> 5; matrix products, arithmetic and copies ran while one was open for 23% -> 20% of each run, Pallas kernels for 9% -> 7%
where the time goes in v5:
time: 129 us; the launch traced here: 128 us
  waiting for transfers between devices  31.6 us (24%)
  blocking collectives  28.5 us (22%)
  Pallas kernels  23.7 us (18%)
  local copies, waits for them, and re-layouts  14.9 us (12%)
  matrix products  14.7 us (11%)
  starting transfers between devices  14.1 us (11%)
    ppermute x10, waiting for transfers between devices, swap(): return lax.ppermute(value, 'aux', [(i, i ^ d) for i in range(dests)])  28.9 us
    all_to_all x1, blocking collectives, local(): lax.all_to_all(mine, ('aux', 'chip'), split_axis=0, concat_axis=0, tiled=...  28.5 us
    dot_general x1, matrix products, local(): jnp.einsum('qbzit,bnt->bqizn', target.reshape(NAUX, blocks, 2, pairs, SIG...  14.7 us
    ppermute x10, starting transfers between devices, swap(): return lax.ppermute(value, 'aux', [(i, i ^ d) for i in range(dests)])  14 us
    pallas_call x3, Pallas kernels, local(): running = respond(*inputs, columns)  13.5 us
    pallas_call x1, Pallas kernels, local(): pl.pallas_call(functools.partial(half_kernel, dests), out_shape=[jax.Shap...  10.2 us
    reshape x1, local copies, waits for them, and re-layouts, local(): columns = jnp.einsum('qbzit,bnt->bqizn', target.reshape(NAUX, blocks, 2,...  6.29 us
    convert_element_type x1, local copies, waits for them, and re-layouts, local(): columns = jnp.einsum('qbzit,bnt->bqizn', target.reshape(NAUX, blocks, 2,...  4.88 us
  transfers between devices with their start and end apart: 11, of which 5 were waited for; matrix products, arithmetic and copies ran while one was open for 20% of the time, Pallas kernels for 7%

profile of v5, /device:TPU:0, one launch (start us, length us, event | category | flops | bytes accessed | tf_op | source)
XLA Modules:
  0.0 128.2 jit_solution(11912646437272881650)
XLA Ops:
  0.0 10.2 %half.1 = (bf16[520,512]{1,0:T(8,128)(2,1)}, bf16[520,512]{1,0:T(8,128)(2,1)}, bf16[520,512]{1,0:T(8,128)(2,1)}, bf16[520,512]{1,0:T(8,128)(2,1)}, bf16[520,512]...) custom-call(s32[2]{0:T(128)} %bitcast.16, s32[2,16]{1,0:T(2,128)} %cost.1, ...), custom_call_target="tpu_custom_call" | custom-call | flops 2000000000 | bytes 20000000 | tf_op jit(solution)/shard_map/half/pallas_call | solution.py:227
  10.2 0.1 collective-permute-start.1
  10.3 3.5 %collective-permute-start.3 = (bf16[520,512]{1,0:T(8,128)(2,1)}, bf16[520,512]{1,0:T(8,128)(2,1)}, u32[]{:S(2)}, u32[]{:S(2)}) collective-permute-start(bf16[520,512]{1,0:T(8,128)(2,1)} %get-tuple-element.17), channel_id=1, source_target_pairs={{0,16},{16,0},{32,48},{48,32},{64,80},{80,64},{96,112},{112,96},{1... | collective-permute-start | bytes 1597448 | tf_op jit(solution)/shard_map/ppermute | solution.py:247
  13.8 0.1 collective-permute-start.5
  13.9 0.7 collective-permute-start.7
  14.6 3.4 %collective-permute-start.8 = (bf16[520,512]{1,0:T(8,128)(2,1)}, bf16[520,512]{1,0:T(8,128)(2,1)S(1)}, u32[]{:S(2)}, u32[]{:S(2)}) collective-permute-start(bf16[520,512]{1,0:T(8,128)(2,1)} %get-tuple-element.21), channel_id=1, source_target_pairs={{0,96},{16,112},{32,64},{48,80},{64,32},{80,48},{96,0},{112,16},{1... | collective-permute-start | bytes 1597448 | tf_op jit(solution)/shard_map/ppermute | solution.py:247
  18.1 8.9 %collective-permute-done.1 = bf16[520,512]{1,0:T(8,128)(2,1)S(1)} collective-permute-done((bf16[520,512]{1,0:T(8,128)(2,1)}, bf16[520,512]{1,0:T(8,128)(2,1)S(1)}, u32[]{:S(2)}, u32[]{:S(2)}) %collective-permute-start.1) | collective-permute-done | bytes 532512 | tf_op jit(solution)/shard_map/ppermute | solution.py:247
  27.0 0.0 collective-permute-start.9
  27.0 0.8 copy-done.4
  27.8 10.7 %collective-permute-done.3 = bf16[520,512]{1,0:T(8,128)(2,1)} collective-permute-done((bf16[520,512]{1,0:T(8,128)(2,1)}, bf16[520,512]{1,0:T(8,128)(2,1)}, u32[]{:S(2)}, u32[]{:S(2)}) %collective-permute-start.3) | collective-permute-done | bytes 532512 | tf_op jit(solution)/shard_map/ppermute | solution.py:247
  38.5 8.1 %collective-permute-done.5 = bf16[520,512]{1,0:T(8,128)(2,1)} collective-permute-done((bf16[520,512]{1,0:T(8,128)(2,1)}, bf16[520,512]{1,0:T(8,128)(2,1)}, u32[]{:S(2)}, u32[]{:S(2)}) %collective-permute-start.5) | collective-permute-done | bytes 532512 | tf_op jit(solution)/shard_map/ppermute | solution.py:247
  46.7 0.6 collective-permute-start.6
  47.3 14.7 %convert_bitcast_fusion = bf16[2,1024,8,2,64]{1,4,2,3,0:T(8,128)(2,1)} fusion(bf16[1024,2,2,8,128]{4,3,2,1,0:T(8,128)(2,1)} %bitcast.14, bf16[2,64,128]{2,1,0:T(8,128)(2,1)S(1)} %copy-done), kind=kOutput, calls=%fused_computation.2 | convolution fusion | flops 538968064 | bytes 12615680 | tf_op jit(solution)/shard_map/qbzit,bnt->bqizn/dot_general | solution.py:256
  62.0 4.9 %copy.16 = bf16[2,1024,8,2,64]{1,4,3,2,0:T(8,128)(2,1)} copy(bf16[2,1024,8,2,64]{1,4,2,3,0:T(8,128)(2,1)} %convert_bitcast_fusion) | data formatting | bytes 8388608 | tf_op jit(solution)/shard_map/convert_element_type | solution.py:259
  66.9 6.3 %copy.17.rest_4_.rest_3_ = bf16[2,1024,1024]{2,1,0:T(8,128)(2,1)} copy(bf16[2,1024,1024]{1,2,0:T(8,128)(2,1)} %bitcast.13) | data formatting | bytes 8388608 | tf_op jit(solution)/shard_map/reshape | solution.py:259
  73.2 2.6 %collective-permute-start = (bf16[520,512]{1,0:T(8,128)(2,1)}, bf16[520,512]{1,0:T(8,128)(2,1)S(1)}, u32[]{:S(2)}, u32[]{:S(2)}) collective-permute-start(bf16[520,512]{1,0:T(8,128)(2,1)} %get-tuple-element.15), channel_id=1, source_target_pairs={{0,16},{16,0},{32,48},{48,32},{64,80},{80,64},{96,112},{112,96},{1... | collective-permute-start | bytes 1597448 | tf_op jit(solution)/shard_map/ppermute | solution.py:247
  75.8 0.0 collective-permute-done.8.rest_2_
  75.8 2.9 %collective-permute-start.2 = (bf16[520,512]{1,0:T(8,128)(2,1)}, bf16[520,512]{1,0:T(8,128)(2,1)S(1)}, u32[]{:S(2)}, u32[]{:S(2)}) collective-permute-start(bf16[520,512]{1,0:T(8,128)(2,1)} %copy-done.4), channel_id=1, source_target_pairs={{0,96},{16,112},{32,64},{48,80},{64,32},{80,48},{96,0},{112,16},{1... | collective-permute-start | bytes 1597448 | tf_op jit(solution)/shard_map/ppermute | solution.py:247
  78.7 0.0 collective-permute-done.9.rest_3_
  78.7 2.2 %copy-done.1 = bf16[2,1024,1024]{2,1,0:T(8,128)(2,1)S(1)} copy-done((bf16[2,1024,1024]{2,1,0:T(8,128)(2,1)S(1)}, bf16[2,1024,1024]{2,1,0:T(8,128)(2,1)}, u32[]{:S(2)}) %copy-start.1) | copy-done | bytes 4194328
  80.9 5.5 %shard_map.73.rest_2_ = f32[8,1032,128]{2,1,0:T(8,128)S(1)} custom-call(bf16[520,512]{1,0:T(8,128)(2,1)S(1)} %copy-done.3, bf16[520,512]{1,0:T(8,128)(2,1)S(1)} %collective-permute-done.7.rest_1_, bf16[520,512]{1,0:T(8,128)(2,1)S(1)} %collective-permute-done.8.rest_2_, bf16[520,512]{1,0:T(8,128)(2,1)S(1)} %collective-permute-done.9.rest_3_, ...), custom_call_target="tpu_custom_call" | custom-call | flops 3000000000 | bytes 10000000 | tf_op jit(solution)/shard_map/pallas_call | solution.py:297
  86.4 0.0 collective-permute-done.4.rest_0_
  86.5 3.4 %shard_map.74.rest_3_ = f32[8,1032,128]{2,1,0:T(8,128)S(1)} custom-call(bf16[520,512]{1,0:T(8,128)(2,1)S(1)} %collective-permute-done.4.rest_0_, bf16[520,512]{1,0:T(8,128)(2,1)S(1)} %collective-permute-done.6.rest_1_, f32[8,1032,128]{2,1,0:T(8,128)S(1)} %shard_map.73.rest_2_, bf16[2,1024,1024]{2,1,0:T(8,128)(2,1)S(1)} %copy-done.2), custom_call_target="tpu_custom_call" | custom-call | flops 3000000000 | bytes 10000000 | tf_op jit(solution)/shard_map/pallas_call | solution.py:297
  89.9 1.2 collective-permute-done.2.rest_2_
  91.0 4.6 %shard_map.75 = (f32[8,8,64,128]{3,2,1,0:T(8,128)S(1)}, bf16[8,8,64,128]{3,2,1,0:T(8,128)(2,1)S(1)}) custom-call(s32[1]{0:T(128)} %bitcast.rest_0_, bf16[520,512]{1,0:T(8,128)(2,1)S(1)} %collective-permute-done.rest_1_, bf16[520,512]{1,0:T(8,128)(2,1)S(1)} %collective-permute-done.2.rest_2_, f32[8,1032,128]{2,1,0:T(8,128)S(1)} %shard_map.74.rest_3_, ...), custom_call_target="tpu_custom_call" | custom-call | flops 3000000000 | bytes 10000000 | tf_op jit(solution)/shard_map/pallas_call | solution.py:297
  95.6 0.1 collective-permute-start.10
  95.7 2.6 %collective-permute-done.10 = bf16[8,8,64,128]{3,2,1,0:T(8,128)(2,1)S(1)} collective-permute-done((bf16[8,8,64,128]{3,2,1,0:T(8,128)(2,1)S(1)}, bf16[8,8,64,128]{3,2,1,0:T(8,128)(2,1)S(1)}, u32[]{:S(2)}, u32[]{:S(2)}) %collective-permute-start.10) | collective-permute-done | bytes 1048608 | tf_op jit(solution)/shard_map/ppermute | solution.py:299
  98.4 0.4 add_convert_fusion
  98.7 28.5 %all_to_all.5 = bf16[64,64,128]{2,1,0:T(8,128)(2,1)S(1)} all-to-all(bf16[64,64,128]{2,1,0:T(8,128)(2,1)S(1)} %bitcast.15), channel_id=1, replica_groups=mesh['aux'=8,'chip'=8,'core'=2] {'aux','chip'}, dimensions={0} | all-to-all | bytes 2097152 | tf_op jit(solution)/shard_map/all_to_all | solution.py:301
  127.2 0.2 convert_reduce_fusion
  127.4 0.1 fusion.5
  127.5 0.7 copy.20
  (13 shorter events, 0.0 us)
Async XLA Ops:
  0.0 47.3 %copy-start = (bf16[2,64,128]{2,1,0:T(8,128)(2,1)S(1)}, bf16[2,64,128]{2,1,0:T(8,128)(2,1)}, u32[]{:S(2)}) copy-start(bf16[2,64,128]{2,1,0:T(8,128)(2,1)} %param.12) | copy-start | bytes 98308
  10.2 16.8 %collective-permute-start.1 = (bf16[520,512]{1,0:T(8,128)(2,1)}, bf16[520,512]{1,0:T(8,128)(2,1)S(1)}, u32[]{:S(2)}, u32[]{:S(2)}) collective-permute-start(bf16[520,512]{1,0:T(8,128)(2,1)} %get-tuple-element.16), channel_id=1, source_target_pairs={{0,16},{16,0},{32,48},{48,32},{64,80},{80,64},{96,112},{112,96},{1... | collective-permute-start | bytes 1597448 | tf_op jit(solution)/shard_map/ppermute | solution.py:247
  10.3 28.2 %collective-permute-start.3 = (bf16[520,512]{1,0:T(8,128)(2,1)}, bf16[520,512]{1,0:T(8,128)(2,1)}, u32[]{:S(2)}, u32[]{:S(2)}) collective-permute-start(bf16[520,512]{1,0:T(8,128)(2,1)} %get-tuple-element.17), channel_id=1, source_target_pairs={{0,16},{16,0},{32,48},{48,32},{64,80},{80,64},{96,112},{112,96},{1... | collective-permute-start | bytes 1597448 | tf_op jit(solution)/shard_map/ppermute | solution.py:247
  13.8 32.8 %collective-permute-start.5 = (bf16[520,512]{1,0:T(8,128)(2,1)}, bf16[520,512]{1,0:T(8,128)(2,1)}, u32[]{:S(2)}, u32[]{:S(2)}) collective-permute-start(bf16[520,512]{1,0:T(8,128)(2,1)} %get-tuple-element.18), channel_id=1, source_target_pairs={{0,16},{16,0},{32,48},{48,32},{64,80},{80,64},{96,112},{112,96},{1... | collective-permute-start | bytes 1597448 | tf_op jit(solution)/shard_map/ppermute | solution.py:247
  13.9 59.2 %collective-permute-start.7 = (bf16[520,512]{1,0:T(8,128)(2,1)}, bf16[520,512]{1,0:T(8,128)(2,1)S(1)}, u32[]{:S(2)}, u32[]{:S(2)}) collective-permute-start(bf16[520,512]{1,0:T(8,128)(2,1)} %get-tuple-element.20), channel_id=1, source_target_pairs={{0,32},{16,48},{32,0},{48,16},{64,96},{80,112},{96,64},{112,80},{1... | collective-permute-start | bytes 1597448 | tf_op jit(solution)/shard_map/ppermute | solution.py:247
  14.6 61.2 %collective-permute-start.8 = (bf16[520,512]{1,0:T(8,128)(2,1)}, bf16[520,512]{1,0:T(8,128)(2,1)S(1)}, u32[]{:S(2)}, u32[]{:S(2)}) collective-permute-start(bf16[520,512]{1,0:T(8,128)(2,1)} %get-tuple-element.21), channel_id=1, source_target_pairs={{0,96},{16,112},{32,64},{48,80},{64,32},{80,48},{96,0},{112,16},{1... | collective-permute-start | bytes 1597448 | tf_op jit(solution)/shard_map/ppermute | solution.py:247
  27.0 0.8 copy-start.4
  27.0 51.7 %collective-permute-start.9 = (bf16[520,512]{1,0:T(8,128)(2,1)}, bf16[520,512]{1,0:T(8,128)(2,1)S(1)}, u32[]{:S(2)}, u32[]{:S(2)}) collective-permute-start(bf16[520,512]{1,0:T(8,128)(2,1)} %get-tuple-element.22), channel_id=1, source_target_pairs={{0,64},{16,80},{32,96},{48,112},{64,0},{80,16},{96,32},{112,48},{1... | collective-permute-start | bytes 1597448 | tf_op jit(solution)/shard_map/ppermute | solution.py:247
  38.5 47.9 %collective-permute-start.4 = (bf16[520,512]{1,0:T(8,128)(2,1)}, bf16[520,512]{1,0:T(8,128)(2,1)S(1)}, u32[]{:S(2)}, u32[]{:S(2)}) collective-permute-start(bf16[520,512]{1,0:T(8,128)(2,1)} %collective-permute-done.3), channel_id=1, source_target_pairs={{0,64},{16,80},{32,96},{48,112},{64,0},{80,16},{96,32},{112,48},{1... | collective-permute-start | bytes 1597448 | tf_op jit(solution)/shard_map/ppermute | solution.py:247
  46.7 39.8 %collective-permute-start.6 = (bf16[520,512]{1,0:T(8,128)(2,1)}, bf16[520,512]{1,0:T(8,128)(2,1)S(1)}, u32[]{:S(2)}, u32[]{:S(2)}) collective-permute-start(bf16[520,512]{1,0:T(8,128)(2,1)} %collective-permute-done.5), channel_id=1, source_target_pairs={{0,32},{16,48},{32,0},{48,16},{64,96},{80,112},{96,64},{112,80},{1... | collective-permute-start | bytes 1597448 | tf_op jit(solution)/shard_map/ppermute | solution.py:247
  66.9 11.8 %copy-start.3 = (bf16[520,512]{1,0:T(8,128)(2,1)S(1)}, bf16[520,512]{1,0:T(8,128)(2,1)}, u32[]{:S(2)}) copy-start(bf16[520,512]{1,0:T(8,128)(2,1)} %get-tuple-element.19.rest_0_) | copy-start | bytes 1597444
  73.2 16.7 %collective-permute-start = (bf16[520,512]{1,0:T(8,128)(2,1)}, bf16[520,512]{1,0:T(8,128)(2,1)S(1)}, u32[]{:S(2)}, u32[]{:S(2)}) collective-permute-start(bf16[520,512]{1,0:T(8,128)(2,1)} %get-tuple-element.15), channel_id=1, source_target_pairs={{0,16},{16,0},{32,48},{48,32},{64,80},{80,64},{96,112},{112,96},{1... | collective-permute-start | bytes 1597448 | tf_op jit(solution)/shard_map/ppermute | solution.py:247
  75.8 15.2 %collective-permute-start.2 = (bf16[520,512]{1,0:T(8,128)(2,1)}, bf16[520,512]{1,0:T(8,128)(2,1)S(1)}, u32[]{:S(2)}, u32[]{:S(2)}) collective-permute-start(bf16[520,512]{1,0:T(8,128)(2,1)} %copy-done.4), channel_id=1, source_target_pairs={{0,96},{16,112},{32,64},{48,80},{64,32},{80,48},{96,0},{112,16},{1... | collective-permute-start | bytes 1597448 | tf_op jit(solution)/shard_map/ppermute | solution.py:247
  78.7 2.2 %copy-start.1 = (bf16[2,1024,1024]{2,1,0:T(8,128)(2,1)S(1)}, bf16[2,1024,1024]{2,1,0:T(8,128)(2,1)}, u32[]{:S(2)}) copy-start(bf16[2,1024,1024]{2,1,0:T(8,128)(2,1)} %copy.17.rest_4_.rest_3_) | copy-start | bytes 12582916
  80.9 5.5 %copy-start.2 = (bf16[2,1024,1024]{2,1,0:T(8,128)(2,1)S(1)}, bf16[2,1024,1024]{2,1,0:T(8,128)(2,1)}, u32[]{:S(2)}) copy-start(bf16[2,1024,1024]{2,1,0:T(8,128)(2,1)} %copy.17.rest_4_.rest_3_) | copy-start | bytes 12582916
  95.6 2.7 %collective-permute-start.10 = (bf16[8,8,64,128]{3,2,1,0:T(8,128)(2,1)S(1)}, bf16[8,8,64,128]{3,2,1,0:T(8,128)(2,1)S(1)}, u32[]{:S(2)}, u32[]{:S(2)}) collective-permute-start(bf16[8,8,64,128]{3,2,1,0:T(8,128)(2,1)S(1)} %get-tuple-element.24), channel_id=1, source_target_pairs={{0,1},{1,0},{2,3},{3,2},{4,5},{5,4},{6,7},{7,6},{8,9},{9,8},{10,11... | collective-permute-start | bytes 3145736 | tf_op jit(solution)/shard_map/ppermute | solution.py:299
